TPU v7x, 512 devices: a whole 4x8x8 slice. The times are simulated.
512 devices in a mesh: dom: 32 (over y, x_hi, core), band: 16 (over z, x_lo).
Axes of the slice: x: 4 (x_hi: 2, x_lo: 2; x = x_hi * 2 + x_lo), y: 8, z: 8, core: 2. Of those that a mesh axis runs over, the one named last changes fastest.
Arguments:
- psi: float32 [512, 192, 512], P('band', 'dom'), may hold values from -40 to 40, as said below
- potential: float32 [192, 512], P('dom'), may hold values from -3 to 1
Outputs:
- filtered_basis: float32 [512, 192, 512], P('band', 'dom')
Inputs may be any that keep to these rules, and one draw needn't show every extreme that they name: `psi`: real-valued band functions.
All inputs are finite; a program needn't handle non-finite values.
Results may differ from a plain program's by a relative error of at most 0.0002.
Values sent between devices are 32-bit elements; how exact they have to be, the bound alone decides.
No kernel may reach another device: no remote copies, remote signals or barrier semaphores. Data moves between devices by JAX's collectives and lax.ppermute only.
A program may use at most 64 MiB of HBM per device.

v0:
```python
import jax
import jax.numpy as jnp
from jax import lax
from jax.sharding import PartitionSpec as P

LX = 32
DEG = 4


COEF = (
    -5369.0 / 1800.0,
    12.0 / 7.0,
    -15.0 / 56.0,
    10.0 / 189.0,
    -1.0 / 112.0,
    2.0 / 1925.0,
    -1.0 / 16632.0,
)
INV_SPACING2 = 4.0
CENTRE = 24.0
HALF_WIDTH = 20.0


def with_halo(block, sides, width):
    for axis, dim in sides:
        count = lax.axis_size(axis)
        forward = [(i, i + 1) for i in range(count - 1)]
        backward = [(target, source) for source, target in forward]
        low = lax.ppermute(
            lax.slice_in_dim(block, block.shape[dim] - width, None, axis=dim), axis, forward
        )
        high = lax.ppermute(lax.slice_in_dim(block, 0, width, axis=dim), axis, backward)
        block = jnp.concatenate([low, block, high], axis=dim)
    return block


def shift_x(values, step):
    amount = step % LX
    column = lax.broadcasted_iota(jnp.int32, values.shape, 2) % LX
    return jnp.where(
        column >= amount, jnp.roll(values, amount, 2), jnp.roll(values, amount - LX, 2)
    )


def shift_y(values, step):
    return jnp.roll(values, step * LX, 2)


def hamiltonian(values, potential):
    depth = values.shape[1]
    padded = with_halo(values, (("dom", 1),), 6)
    summed = 3.0 * COEF[0] * values
    for step in range(1, 7):
        beside_all = shift_x(values, step) + shift_x(values, -step)
        beside_all = beside_all + shift_y(values, step) + shift_y(values, -step)
        beside_all = (
            beside_all
            + padded[:, 6 + step : 6 + step + depth]
            + padded[:, 6 - step : 6 - step + depth]
        )
        summed = summed + COEF[step] * beside_all
    return -0.5 * INV_SPACING2 * summed + potential[None] * values


def chebyshev(start, potential):
    previous = start
    current = (hamiltonian(start, potential) - CENTRE * start) / HALF_WIDTH
    for degree in range(1, DEG):
        following = (
            2.0 * (hamiltonian(current, potential) - CENTRE * current) / HALF_WIDTH - previous
        )
        previous, current = (current, following)
    return current


def inverse_rows(gram, all_bands, tile_bands):
    lower = jnp.linalg.cholesky(gram)
    inverse = lax.linalg.triangular_solve(
        lower, jnp.eye(all_bands, dtype=jnp.float32), left_side=True, lower=True
    )
    return lax.dynamic_slice_in_dim(inverse, lax.axis_index("band") * tile_bands, tile_bands, 0)


def shards(psi, potential):
    filtered = chebyshev(psi, potential)
    tile_bands = psi.shape[0]
    points_dev = psi.shape[1] * psi.shape[2]
    all_points = points_dev * lax.axis_size("dom")
    all_bands = tile_bands * lax.axis_size("band")
    flatrows = filtered.reshape(tile_bands, points_dev)
    piece = lax.all_gather(filtered, "band", axis=0, tiled=True)
    count = piece.shape[0]
    contrib = jnp.dot(
        flatrows,
        piece.reshape(count, points_dev).T,
        precision=lax.Precision.HIGHEST,
        preferred_element_type=jnp.float32,
    )
    gram_rows = lax.psum(contrib, "dom") / all_points
    gram = lax.all_gather(gram_rows, "band", axis=0, tiled=True)
    my_rows = inverse_rows(gram, all_bands, tile_bands)
    piece = lax.all_gather(filtered, "band", axis=0, tiled=True)
    count = piece.shape[0]
    rotated = jnp.dot(
        my_rows,
        piece.reshape(count, points_dev),
        precision=lax.Precision.HIGHEST,
        preferred_element_type=jnp.float32,
    )
    return rotated.reshape(psi.shape)


def solution(mesh):
    placed = (P("band", "dom", None), P("dom", None))
    return jax.shard_map(
        shards, mesh=mesh, in_specs=placed, out_specs=P("band", "dom", None), check_vma=False
    )
```

profile of v0, /device:TPU:6, one launch (start us, length us, event | category | flops | bytes accessed | tf_op | source)
XLA Modules:
  0.0 725.2 jit_solution(7436480236359161126)
XLA Ops:
  6.5 2.0 collective-permute-start.1
  8.6 5.1 collective-permute-start
  23.2 3.9 broadcast_multiply_fusion
  31.5 1.9 collective-permute-start.2
  33.4 2.6 collective-permute-start.3
  36.3 2.4 collective-permute-done.2
  38.7 8.4 %collective-permute-done.3 = f32[32,6,512]{2,0,1:T(8,128)S(1)} collective-permute-done((f32[32,6,512]{2,0,1:T(8,128)S(1)}, f32[32,6,512]{2,0,1:T(8,128)S(1)}, u32[]{:S(2)}, u32[]{:S(2)}) %collective-permute-start.3) | collective-permute-done | bytes 393248 | tf_op jit(solution)/shard_map/ppermute | solution.py:29
  47.1 3.8 fusion.80
  53.7 1.9 collective-permute-start.4
  55.6 2.4 collective-permute-start.5
  60.9 6.2 collective-permute-done.5
  67.1 3.8 fusion.92
  73.7 1.9 collective-permute-start.6
  75.7 2.8 collective-permute-start.7
  80.9 6.3 collective-permute-done.7
  87.3 4.5 fusion.104
  91.8 150.9 %all-gather.3.cloned.1.call-done = f32[512,6,512]{2,0,1:T(8,128)} async-done(((f32[32,6,512]{2,0,1:T(8,128)}), f32[512,6,512]{2,0,1:T(8,128)}) %all-gather.3.cloned.1.call-update) | async-done | bytes 6291472 | tf_op jit(solution)/shard_map/all_gather | solution.py:91
  242.7 9.3 %convolution_bitcast_fusion = f32[32,512]{1,0:T(8,128)} fusion(f32[32,6,512]{2,0,1:T(8,128)} %fusion.104, f32[512,6,512]{2,0,1:T(8,128)} %all-gather.3.cloned.1.call-done), kind=kOutput, calls=%fused_computation.72 | convolution fusion | flops 603979776 | bytes 6750208 | tf_op jit(solution)/shard_map/dot_general | solution.py:93
  252.0 242.1 %all-reduce.3.cloned.1.call-done = f32[32,512]{1,0:T(8,128)} async-done(((f32[32,512]{1,0:T(8,128)}), f32[32,512]{1,0:T(8,128)}) %all-reduce.3.cloned.1.call-update) | async-done | bytes 65552 | tf_op jit(solution)/shard_map/psum | solution.py:99
  496.6 6.7 copy.9
  503.3 65.1 %all-gather.5.cloned.1.call-done = f32[512,512]{1,0:T(8,128)} async-done(((f32[32,512]{1,0:T(8,128)}), f32[512,512]{1,0:T(8,128)}) %all-gather.5.cloned.1.call-update) | async-done | bytes 1048592 | tf_op jit(solution)/shard_map/all_gather | solution.py:100
  571.4 11.7 %cholesky.104 = f32[128,128]{1,0:T(8,128)S(1)} custom-call(f32[128,128]{1,0:T(8,128)S(1)} %cholesky.266), custom_call_target="Cholesky" | custom-call | tf_op jit(solution)/shard_map/jit(cholesky)/cholesky | solution.py:77
  583.3 9.8 %custom-call.30 = f32[1,128,128]{1,2,0:T(8,128)S(1)} custom-call(f32[1,128,128]{2,1,0:T(8,128)S(1)} %get-tuple-element.324), custom_call_target="InvertDiagBlocksLowerTriangular" | custom-call | tf_op jit(solution)/shard_map/jit(cholesky)/cholesky | solution.py:77
  593.8 11.7 %cholesky.217 = f32[128,128]{1,0:T(8,128)S(1)} custom-call(f32[128,128]{1,0:T(8,128)S(1)} %cholesky.270), custom_call_target="Cholesky" | custom-call | tf_op jit(solution)/shard_map/jit(cholesky)/cholesky | solution.py:77
  605.5 10.0 %custom-call.31 = f32[1,128,128]{1,2,0:T(8,128)S(1)} custom-call(f32[1,128,128]{2,1,0:T(8,128)S(1)} %get-tuple-element.321), custom_call_target="InvertDiagBlocksLowerTriangular" | custom-call | tf_op jit(solution)/shard_map/jit(cholesky)/cholesky | solution.py:77
  616.2 11.7 %cholesky.238 = f32[128,128]{1,0:T(8,128)S(1)} custom-call(f32[128,128]{1,0:T(8,128)S(1)} %cholesky.275), custom_call_target="Cholesky" | custom-call | tf_op jit(solution)/shard_map/jit(cholesky)/cholesky | solution.py:77
  628.5 9.8 %custom-call.32 = f32[1,128,128]{1,2,0:T(8,128)S(1)} custom-call(f32[1,128,128]{2,1,0:T(8,128)S(1)} %get-tuple-element.318), custom_call_target="InvertDiagBlocksLowerTriangular" | custom-call | tf_op jit(solution)/shard_map/jit(cholesky)/cholesky | solution.py:77
  639.0 11.7 %cholesky.255 = f32[128,128]{1,0:T(8,128)S(1)} custom-call(f32[128,128]{1,0:T(8,128)S(1)} %convolution_subtract_fusion.5), custom_call_target="Cholesky" | custom-call | tf_op jit(solution)/shard_map/jit(cholesky)/cholesky | solution.py:77
  654.7 10.3 %while.1 = (s32[]{:T(128)}, f32[512,512]{1,0:T(8,128)S(1)}, s32[4,2]{0,1:T(2,128)S(1)}, f32[4,128,128]{2,1,0:T(8,128)}, s32[]{:T(128)}) while((s32[]{:T(128)}, f32[512,512]{1,0:T(8,128)S(1)}, s32[4,2]{0,1:T(2,128)S(1)}, f32[4,128,128]{2,1,0:T(8,128)}, s32[]{:T(128)}) %tuple.173), condition=%wide.while_cond, body=%wide.while_body.sunk | while | flops 2 | bytes 132705 | solution.py:78
  658.1 1.9 bitcast_dynamic-update-slice_fusion.2
  665.0 40.1 %custom-call.33 = f32[4,128,128]{1,2,0:T(8,128)S(1)} custom-call(f32[4,128,128]{2,1,0:T(8,128)} %get-tuple-element.12), custom_call_target="InvertDiagBlocksLowerTriangular" | custom-call | tf_op jit(solution)/shard_map/triangular_solve | solution.py:78
  709.0 9.2 %fusion = f32[32,6,512]{2,0,1:T(8,128)} fusion(f32[512,6,512]{0,2,1:T(8,128)} %copy.9, s32[]{:T(128)S(6)} %select_n.397, f32[128,512]{1,0:T(8,128)S(1)} %fusion.271, f32[128,512]{1,0:T(8,128)S(1)} %fusion.286, f32[128,512]{1,0:T(8,128)S(1)} %fusion.284, f32[128,512]{1,0:T(8,128)S(1)} %fusion.283), kind=kOutput, calls=%fused_computation.2 | convolution fusion | flops 604028928 | bytes 7733252 | tf_op jit(solution)/shard_map/dot_general | solution.py:104
  (209 shorter events, 46.1 us)
Async XLA Ops:
  6.5 12.4 %copy-start = (f32[32,6,512]{2,0,1:T(8,128)S(1)}, f32[32,6,512]{2,0,1:T(8,128)}, u32[]{:S(2)}) copy-start(f32[32,6,512]{2,0,1:T(8,128)} %param.2) | copy-start | bytes 1179652
  6.5 236.2 %all-gather.3.cloned.1.call-start = ((), (), s32[]{:S(2)}) async-start(), calls=%async_computation | async-start | bytes 6684672 | tf_op jit(solution)/shard_map/all_gather | solution.py:91
  6.5 16.4 %collective-permute-start.1 = (f32[32,6,512]{2,0,1:T(8,128)}, f32[32,6,512]{2,0,1:T(8,128)S(1)}, u32[]{:S(2)}, u32[]{:S(2)}) collective-permute-start(f32[32,6,512]{2,0,1:T(8,128)} %param.2), channel_id=1, source_target_pairs={{0,16},{16,32},{32,48},{48,64},{64,80},{80,96},{96,112},{112,128},... | collective-permute-start | bytes 1179656 | tf_op jit(solution)/shard_map/ppermute | solution.py:29
  8.6 14.5 %collective-permute-start = (f32[32,6,512]{2,0,1:T(8,128)}, f32[32,6,512]{2,0,1:T(8,128)S(1)}, u32[]{:S(2)}, u32[]{:S(2)}) collective-permute-start(f32[32,6,512]{2,0,1:T(8,128)} %param.2), channel_id=1, source_target_pairs={{16,0},{32,16},{48,32},{64,48},{80,64},{96,80},{112,96},{128,112},... | collective-permute-start | bytes 1179656 | tf_op jit(solution)/shard_map/ppermute | solution.py:32
  20.7 2.2 copy-start.1
  31.5 7.2 collective-permute-start.2
  33.4 13.7 %collective-permute-start.3 = (f32[32,6,512]{2,0,1:T(8,128)S(1)}, f32[32,6,512]{2,0,1:T(8,128)S(1)}, u32[]{:S(2)}, u32[]{:S(2)}) collective-permute-start(f32[32,6,512]{2,0,1:T(8,128)S(1)} %get-tuple-element.21), channel_id=1, source_target_pairs={{0,16},{16,32},{32,48},{48,64},{64,80},{80,96},{96,112},{112,128},... | collective-permute-start | bytes 1179656 | tf_op jit(solution)/shard_map/ppermute | solution.py:29
  53.7 7.2 collective-permute-start.4
  55.6 11.5 %collective-permute-start.5 = (f32[32,6,512]{2,0,1:T(8,128)S(1)}, f32[32,6,512]{2,0,1:T(8,128)S(1)}, u32[]{:S(2)}, u32[]{:S(2)}) collective-permute-start(f32[32,6,512]{2,0,1:T(8,128)S(1)} %fusion.80), channel_id=1, source_target_pairs={{0,16},{16,32},{32,48},{48,64},{64,80},{80,96},{96,112},{112,128},... | collective-permute-start | bytes 1179656 | tf_op jit(solution)/shard_map/ppermute | solution.py:29
  73.7 7.2 collective-permute-start.6
  75.7 11.6 %collective-permute-start.7 = (f32[32,6,512]{2,0,1:T(8,128)S(1)}, f32[32,6,512]{2,0,1:T(8,128)S(1)}, u32[]{:S(2)}, u32[]{:S(2)}) collective-permute-start(f32[32,6,512]{2,0,1:T(8,128)S(1)} %fusion.92), channel_id=1, source_target_pairs={{0,16},{16,32},{32,48},{48,64},{64,80},{80,96},{96,112},{112,128},... | collective-permute-start | bytes 1179656 | tf_op jit(solution)/shard_map/ppermute | solution.py:29
  91.7 402.4 %all-reduce.3.cloned.1.call-start = ((), (), s32[]{:S(2)}) async-start(), calls=%async_computation.1 | async-start | bytes 131072 | tf_op jit(solution)/shard_map/psum | solution.py:99
  252.0 316.4 %all-gather.5.cloned.1.call-start = ((), (), s32[]{:S(2)}) async-start(), calls=%async_computation.2 | async-start | bytes 1114112 | tf_op jit(solution)/shard_map/all_gather | solution.py:100
Sparse Core Ops, SparseCore 0:
  91.9 150.8 all-gather.2
  252.1 241.9 all-reduce.2
  496.2 72.0 all-gather.4
where the time goes:
time: 732 us; the launch traced here: 725 us
  waiting for transfers between devices  483 us (66%)
  other arithmetic  139 us (19%)
  local copies, waits for them, and re-layouts  41.3 us (6%)
  matrix products  24.1 us (3%)
  starting transfers between devices  20.9 us (3%)
  between operations  17 us (2%)
    psum x1, waiting for transfers between devices, shards(): gram_rows = lax.psum(contrib, 'dom') / all_points  242 us
    all_gather x1, waiting for transfers between devices, shards(): piece = lax.all_gather(filtered, 'band', axis=0, tiled=True)  151 us
    another operation x14, other arithmetic, inverse_rows(): lower = jnp.linalg.cholesky(gram)  78.6 us
    all_gather x1, waiting for transfers between devices, shards(): gram = lax.all_gather(gram_rows, 'band', axis=0, tiled=True)  65.1 us
    another operation x3, other arithmetic, inverse_rows(): lax.linalg.triangular_solve(lower, jnp.eye(all_bands, dtype=jnp.float32),...  40.3 us
    ppermute x4, waiting for transfers between devices, with_halo(): lax.ppermute(lax.slice_in_dim(block, block.shape[dim] - width, None, axis...  20.9 us
  transfers between devices with their start and end apart: 11, of which 9 were waited for; matrix products, arithmetic and copies ran while one was open for 3% of the time, Pallas kernels for 0%

commit v1 on v0

v1 whole, which is shorter than its diff:
```python
import jax
import jax.numpy as jnp
import numpy as np
from jax import lax
from jax.experimental import pallas as pl
from jax.experimental.pallas import tpu as pltpu
from jax.sharding import PartitionSpec as P

NB = 512
LX = 32
LY = 16
NZ = 192
CELLS = LX * LY
NPTS = NZ * CELLS
DEG = 4
DOM = 32
BAND = 16
TILE = NB // BAND
DEPTH = NZ // DOM
LANES = 128
ALL = ("band", "dom")

COEF = (
    -5369.0 / 1800.0,
    12.0 / 7.0,
    -15.0 / 56.0,
    10.0 / 189.0,
    -1.0 / 112.0,
    2.0 / 1925.0,
    -1.0 / 16632.0,
)
INV_SPACING2 = 4.0
CENTRE = 24.0
HALF_WIDTH = 20.0

HIGHEST = lax.Precision.HIGHEST
f32 = jnp.float32
bf16 = jnp.bfloat16


def split_constant(matrix):
    pieces = []
    rest = matrix.astype(np.float64)
    for _ in range(3):
        piece = rest.astype(np.float32).astype(bf16)
        pieces.append(piece)
        rest = rest - piece.astype(np.float64)
    return pieces


def plane_matrix():
    out = np.zeros((CELLS, CELLS))
    scale = -0.5 * INV_SPACING2 / HALF_WIDTH
    for y in range(LY):
        for x in range(LX):
            row = y * LX + x
            out[row, row] += scale * 3.0 * COEF[0] - CENTRE / HALF_WIDTH
            for k in range(1, 7):
                for step in (k, -k):
                    out[row, y * LX + (x + step) % LX] += scale * COEF[k]
                    out[row, (y + step) % LY * LX + x] += scale * COEF[k]
    return out


def layer_matrix():
    out = np.zeros((NZ, NZ))
    scale = -0.5 * INV_SPACING2 / HALF_WIDTH
    for k in range(1, 7):
        out += scale * COEF[k] * (np.eye(NZ, k=k) + np.eye(NZ, k=-k))
    return out


def split_value(value):
    high = value.astype(bf16)
    rest = value - high.astype(f32)
    middle = rest.astype(bf16)
    low = (rest - middle.astype(f32)).astype(bf16)
    return high, middle, low


def dot_split(left, right):
    def dot(a, b):
        return jnp.dot(a, b, preferred_element_type=f32)

    small = dot(left[0], right[2]) + dot(left[1], right[1]) + dot(left[2], right[0])
    return (small + (dot(left[0], right[1]) + dot(left[1], right[0]))) + dot(left[0], right[0])


def pack_kernel(psi, potential, out):
    for layer in range(DEPTH):
        for quarter in range(4):
            lanes = slice(quarter * LANES, (quarter + 1) * LANES)
            row = layer * 8 + quarter
            out[pl.ds(row, TILE, stride=8 * DEPTH), :] = psi[layer, :, lanes]
            out[pl.ds(row + 4, TILE, stride=8 * DEPTH), :] = jnp.broadcast_to(
                potential[layer : layer + 1, lanes] * (1.0 / HALF_WIDTH), (TILE, LANES)
            )


def filter_kernel(rows, m0, m1, m2, v0, v1, v2, out, scratch):
    start = jnp.concatenate([rows[pl.ds(q, NZ, stride=8), :] for q in range(4)], axis=1)
    potential = jnp.concatenate([rows[pl.ds(4 + q, NZ, stride=8), :] for q in range(4)], axis=1)
    plane = (m0[...], m1[...], m2[...])
    layers = (v0[...], v1[...], v2[...])

    def apply(values):
        pieces = split_value(values)
        return dot_split(pieces, plane) + dot_split(layers, pieces) + potential * values

    previous = start
    current = apply(start)
    for _ in range(1, DEG):
        previous, current = current, 2.0 * apply(current) - previous
    norm = jnp.sum(jnp.sum(current * current, axis=0, keepdims=True), axis=1, keepdims=True) * (
        1.0 / NPTS
    )
    for quarter in range(4):
        scratch[quarter * NZ : (quarter + 1) * NZ, :] = current[
            :, quarter * LANES : (quarter + 1) * LANES
        ]
    lane = lax.broadcasted_iota(jnp.int32, (DOM, LANES), 1)
    norms = jnp.broadcast_to(norm, (DOM, LANES))
    for piece in range(BAND):
        first = scratch[pl.ds((piece % 4) * NZ + piece // 4, DOM, stride=DEPTH), :]
        half = piece // 2
        second = scratch[pl.ds((half % 4) * NZ + 4 + half // 4, DOM, stride=DEPTH), :]
        valid = lane < 64 if piece % 2 == 0 else lane >= 64
        out[pl.ds(piece * 2 * DOM, DOM, stride=2), :] = first
        out[pl.ds(piece * 2 * DOM + 1, DOM, stride=2), :] = jnp.where(valid, second, norms)


def points_of(rows, odd):
    first = rows[pl.ds(0, NB, stride=2), :]
    second = rows[pl.ds(1, NB, stride=2), :]
    upper = (lax.broadcasted_iota(jnp.int32, (NB, LANES), 1) >= 64).astype(jnp.int32)
    return first, jnp.where(upper == odd, second, 0.0), second


def dot_nt(a, b):
    return lax.dot_general(
        a, b, (((1,), (1,)), ((), ())), precision=HIGHEST, preferred_element_type=f32
    )


def dot_nn(a, b):
    return jnp.dot(a, b, precision=HIGHEST, preferred_element_type=f32)


def gram_kernel(odd, rows, out):
    first, second, _ = points_of(rows, odd[0])
    points = jnp.concatenate([first, second], axis=1)
    low, high = points[:256], points[256:]
    row = lax.broadcasted_iota(jnp.int32, (256, 256), 0)
    col = lax.broadcasted_iota(jnp.int32, (256, 256), 1)
    folded = jnp.where(col <= row, dot_nt(low, low), dot_nt(high, high))
    below = dot_nt(high, low)
    out[0:256, :] = folded[:, :LANES]
    out[256:512, :] = folded[:, LANES:]
    out[512:768, :] = below[:, :LANES]
    out[768:1024, :] = below[:, LANES:]


def sum_kernel(parts, out):
    total = jnp.sum(parts[...].reshape(8, 16, 8, LANES), axis=0)
    total = jnp.sum(total, axis=0)
    total = total + pltpu.roll(total, 4, 0)
    total = (total + pltpu.roll(total, 2, 0)) * (1.0 / NPTS)
    out[...] = jnp.broadcast_to(total[None], (NB // 4, 8, LANES)).reshape(2 * NB, LANES)


def invert_block(block, inverse):
    full = (8, LANES)
    row = lax.broadcasted_iota(jnp.int32, (LANES, LANES), 0)
    col = lax.broadcasted_iota(jnp.int32, (LANES, LANES), 1)
    inverse[...] = jnp.where(row == col, 1.0, 0.0)
    sub = lax.broadcasted_iota(jnp.int32, full, 0)
    for panel in range(16):
        here = slice(8 * panel, 8 * panel + 8)
        v = block[here, :]
        w = inverse[here, :]
        cols = [
            jnp.broadcast_to(v[:, 8 * panel + t : 8 * panel + t + 1], full) for t in range(8)
        ]
        e = [[None] * 8 for _ in range(8)]
        for t in range(8):
            for s in range(t, 8):
                e[s][t] = jnp.broadcast_to(cols[t][s : s + 1, :], full)
        inv = [None] * 8
        for t in range(8):
            inv[t] = lax.rsqrt(e[t][t])
            for s in range(t + 1, 8):
                e[s][t] = e[s][t] * inv[t]
            for u in range(t + 1, 8):
                for s in range(u, 8):
                    e[s][u] = e[s][u] - e[s][t] * e[u][t]
        ys, zs = [], []
        for s in range(8):
            y = jnp.broadcast_to(v[s : s + 1, :], full)
            z = jnp.broadcast_to(w[s : s + 1, :], full)
            for u in range(s):
                y = y - e[s][u] * ys[u]
                z = z - e[s][u] * zs[u]
            ys.append(y * inv[s])
            zs.append(z * inv[s])
        done = zs[0]
        for s in range(1, 8):
            done = jnp.where(sub == s, zs[s], done)
        inverse[here, :] = done
        if panel == 15:
            break
        for s in reversed(range(8)):
            y, z = ys[s], zs[s]
            for u in range(s + 1, 8):
                y = y - e[u][s] * ys[u]
                z = z - e[u][s] * zs[u]
            ys[s], zs[s] = y * inv[s], z * inv[s]
        for q in range(panel + 1, 16):
            there = slice(8 * q, 8 * q + 8)
            d = block[there, :]
            i = inverse[there, :]
            for t in range(8):
                c = jnp.broadcast_to(block[there, 8 * panel + t : 8 * panel + t + 1], full)
                d = d - c * ys[t]
                i = i - c * zs[t]
            block[there, :] = d
            inverse[there, :] = i


def solve_kernel(odd, gram, rows, out, s_ref, x_ref, block, inverse):
    first, second, raw = points_of(rows, odd[0])
    x_ref[:, :LANES] = first
    x_ref[:, LANES:] = second
    norms = jnp.where(odd[0] == 0, raw[256:, LANES - 1 : LANES], raw[256:, 0:1])
    folded = jnp.concatenate([gram[0:256, :], gram[256:512, :]], axis=1)
    flipped = folded.T
    row = lax.broadcasted_iota(jnp.int32, (256, 256), 0)
    col = lax.broadcasted_iota(jnp.int32, (256, 256), 1)
    s_ref[:256, :256] = jnp.where(col <= row, folded, flipped)
    s_ref[256:, 256:] = jnp.where(
        col == row, jnp.broadcast_to(norms, (256, 256)), jnp.where(col > row, folded, flipped)
    )
    s_ref[256:, :LANES] = gram[512:768, :]
    s_ref[256:, LANES:256] = gram[768:1024, :]
    for j in range(4):
        here = slice(j * LANES, (j + 1) * LANES)
        rest = slice((j + 1) * LANES, NB)
        block[...] = s_ref[here, here]
        invert_block(block, inverse)
        factor_inverse = inverse[...]
        solved = dot_nn(factor_inverse, x_ref[here, :])
        x_ref[here, :] = solved
        if j < 3:
            panel = dot_nt(s_ref[rest, here], factor_inverse)
            x_ref[rest, :] = x_ref[rest, :] - dot_nn(panel, solved)
            s_ref[rest, rest] = s_ref[rest, rest] - dot_nt(panel, panel)
    for tile in range(BAND):
        at = tile * TILE
        out[tile * 48 : tile * 48 + 32, :] = x_ref[at : at + TILE, :LANES]
        out[tile * 48 + 32 : tile * 48 + 48, :] = x_ref[at : at + 16, LANES:] + pltpu.roll(
            x_ref[at + 16 : at + 32, LANES:], 64, 1
        )


def unpack_kernel(rows, out):
    for piece in range(BAND):
        quarter = piece % 4
        out[piece // 4, :, quarter * LANES : (quarter + 1) * LANES] = rows[
            piece * 48 : piece * 48 + 32, :
        ]
    lower = lax.broadcasted_iota(jnp.int32, (16, LANES), 1) < 64
    for half in range(8):
        lanes = slice((half % 4) * LANES, (half % 4 + 1) * LANES)
        even = rows[2 * half * 48 + 32 : 2 * half * 48 + 48, :]
        odd = rows[(2 * half + 1) * 48 + 32 : (2 * half + 1) * 48 + 48, :]
        out[4 + half // 4, 0:16, lanes] = jnp.where(lower, even, odd)
        out[4 + half // 4, 16:32, lanes] = pltpu.roll(jnp.where(lower, odd, even), 64, 1)


def whole():
    return pl.BlockSpec(memory_space=pltpu.VMEM)


def scalar():
    return pl.BlockSpec(memory_space=pltpu.SMEM)


def call(kernel, name, shape, specs, scratch=()):
    return pl.pallas_call(
        kernel,
        name=name,
        out_shape=jax.ShapeDtypeStruct(shape, f32),
        in_specs=specs,
        out_specs=whole(),
        scratch_shapes=list(scratch),
        compiler_params=pltpu.CompilerParams(vmem_limit_bytes=48 << 20),
    )


def do_pack(psi, potential):
    return call(pack_kernel, "pack", (TILE * 8 * DEPTH, LANES), [whole()] * 2)(psi, potential)


def do_filter(rows):
    constants = [jnp.asarray(p) for p in split_constant(plane_matrix())]
    constants += [jnp.asarray(p) for p in split_constant(layer_matrix())]
    return call(
        filter_kernel, "filter", (2 * NB, LANES), [whole()] * 7, [pltpu.VMEM((4 * NZ, LANES), f32)]
    )(rows, *constants)


def do_gram(odd, rows):
    return call(gram_kernel, "gram", (2 * NB, LANES), [scalar(), whole()])(odd, rows)


def do_sum(parts):
    return call(sum_kernel, "sum", (2 * NB, LANES), [whole()])(parts)


def do_solve(odd, gram, rows):
    return call(
        solve_kernel,
        "solve",
        (BAND * 48, LANES),
        [scalar(), whole(), whole()],
        [
            pltpu.VMEM((NB, NB), f32),
            pltpu.VMEM((NB, 2 * LANES), f32),
            pltpu.VMEM((LANES, LANES), f32),
            pltpu.VMEM((LANES, LANES), f32),
        ],
    )(odd, gram, rows)


def do_unpack(rows):
    return call(unpack_kernel, "unpack", (DEPTH, TILE, CELLS), [whole()])(rows)


def exchange(rows, axis, parts):
    shaped = rows.reshape(parts, rows.shape[0] // parts, LANES)
    return lax.all_to_all(shaped, axis, 0, 0).reshape(rows.shape)


def shards(psi, potential):
    odd = (lax.axis_index("band") % 2).astype(jnp.int32).reshape(1)
    bands = exchange(do_pack(jnp.transpose(psi, (1, 0, 2)), potential), "dom", DOM)
    points = exchange(do_filter(bands), ALL, NB)
    parts = exchange(do_gram(odd, points), ALL, NB)
    gram = exchange(do_sum(parts), ALL, NB)
    result = exchange(do_solve(odd, gram, points), "band", BAND)
    return jnp.transpose(do_unpack(result), (1, 0, 2))


def solution(mesh):
    placed = (P("band", "dom", None), P("dom", None))
    return jax.shard_map(
        shards, mesh=mesh, in_specs=placed, out_specs=P("band", "dom", None), check_vma=False
    )
```

time: 732 us -> 190 us (0.26)
  waiting for transfers between devices: 483 us -> 21.7 us
  other arithmetic: 139 us -> 0 us
  blocking collectives: 0 us -> 115 us
  local copies, waits for them, and re-layouts: 41.3 us -> 1.74 us
  Pallas kernels: 0 us -> 33.1 us
  matrix products: 24.1 us -> 0 us
  between operations: 17 us -> 0.11 us
    psum x1 -> x0, waiting for transfers between devices: 242 us -> none  [shards(): gram_rows = lax.psum(contrib, 'dom') / all_points]
    all_gather x2 -> x0, waiting for transfers between devices: 216 us -> none  [the longest x1 151 us: shards(): piece = lax.all_gather(filtered, 'band', axis=0, tiled=True)]
    another operation x17 -> x0, other arithmetic: 119 us -> none  [the longest x14 78.6 us: inverse_rows(): lower = jnp.linalg.cholesky(gram)]
    all_to_all x0 -> x4, blocking collectives: none -> 115 us  [exchange(): return lax.all_to_all(shaped, axis, 0, 0).reshape(rows.shape)]
    pallas_call x0 -> x6, Pallas kernels: none -> 33.1 us  [the longest x1 25.9 us: do_solve(): call(solve_kernel, 'solve', (BAND * 48, LANES), [scalar(), whole(), whole...]
    ppermute x8 -> x0, waiting for transfers between devices: 24.9 us -> none  [the longest x4 20.9 us: with_halo(): lax.ppermute(lax.slice_in_dim(block, block.shape[dim] - width, None, axis...]
    slice x144 -> x0, local copies, waits for them, and re-layouts: 22.7 us -> none  [the longest x48 8.6 us: shift_x(): jnp.roll(values, amount, 2)]
    all_to_all x0 -> x1, waiting for transfers between devices: none -> 21.7 us  [exchange(): return lax.all_to_all(shaped, axis, 0, 0).reshape(rows.shape)]
  transfers between devices with their start and end apart: 11 -> 1, of which waited for: 9 -> 1; matrix products, arithmetic and copies ran while one was open for 3% -> 0% of each run, Pallas kernels for 0% -> 0%
where the time goes in v1:
time: 190 us; the launch traced here: 188 us
  blocking collectives  115 us (61%)
  Pallas kernels  33.1 us (17%)
  waiting for transfers between devices  21.7 us (11%)
  starting transfers between devices  15.9 us (8%)
    all_to_all x4, blocking collectives, exchange(): return lax.all_to_all(shaped, axis, 0, 0).reshape(rows.shape)  115 us
    pallas_call x1, Pallas kernels, do_solve(): call(solve_kernel, 'solve', (BAND * 48, LANES), [scalar(), whole(), whole...  25.9 us
    all_to_all x1, waiting for transfers between devices, exchange(): return lax.all_to_all(shaped, axis, 0, 0).reshape(rows.shape)  21.7 us
    all_to_all x1, starting transfers between devices, exchange(): return lax.all_to_all(shaped, axis, 0, 0).reshape(rows.shape)  15.9 us
    pallas_call x1, Pallas kernels, do_filter(): call(filter_kernel, 'filter', (2 * NB, LANES), [whole()] * 7, [pltpu.VMEM...  5.17 us
  transfers between devices with their start and end apart: 1, of which 1 were waited for; matrix products, arithmetic and copies ran while one was open for 0% of the time, Pallas kernels for 0%

profile of v1, /device:TPU:6, one launch (start us, length us, event | category | flops | bytes accessed | tf_op | source)
XLA Modules:
  0.0 187.7 jit_solution(13788421643258228397)
XLA Ops:
  0.0 0.0 copy-start.3
  0.0 1.0 copy-done.3
  1.0 0.0 copy-start.7
  1.0 0.7 copy-done.7
  1.7 0.0 copy-start.4
  1.7 0.0 copy-start.5
  1.7 0.0 copy-start.6
  1.7 0.3 pack.1
  2.0 0.0 copy-start
  2.1 0.0 copy-start.1
  2.1 0.0 copy-start.2
  2.1 33.4 %all_to_all.25 = f32[32,48,128]{2,1,0:T(8,128)S(1)} all-to-all(f32[32,48,128]{2,1,0:T(8,128)S(1)} %bitcast.15), channel_id=1, replica_groups=mesh['dom'=32,'band'=16] {'dom'}, dimensions={0} | all-to-all | bytes 1572864 | tf_op jit(solution)/shard_map/all_to_all | solution.py:340
  35.5 0.0 copy-done.4
  35.5 0.0 copy-done.5
  35.5 0.0 copy-done.6
  35.5 0.0 copy-done
  35.5 0.0 copy-done.1
  35.6 0.0 copy-done.2
  35.6 5.2 %filter.1 = f32[1024,128]{1,0:T(8,128)} custom-call(f32[1536,128]{1,0:T(8,128)S(1)} %bitcast.16, bf16[512,512]{1,0:T(8,128)(2,1)S(1)} %copy-done.2, bf16[512,512]{1,0:T(8,128)(2,1)S(1)} %copy-done.1, bf16[512,512]{1,0:T(8,128)(2,1)S(1)} %copy-done, bf16[192,192]{1,0:T(8,128)(2,1)S(1)} %copy-done.6, bf16[192,192]{1,0:T(8,128)(2,1)S(1)} %copy-done.5, ...), custom_call_target="tpu_custom_call" | custom-call | tf_op jit(solution)/shard_map/filter/pallas_call | solution.py:306
  40.7 15.9 %all-to-all-start.1 = ((f32[512,2,128]{2,1,0:T(2,128)}), f32[512,2,128]{2,1,0:T(2,128)S(1)}, u32[]{:S(2)}, u32[]{:S(2)}) async-start(f32[512,2,128]{2,1,0:T(2,128)} %bitcast.4), calls=%async_computation.1 | async-start | bytes 1048576 | tf_op jit(solution)/shard_map/all_to_all | solution.py:340
  56.7 21.7 %all-to-all-done.1 = f32[512,2,128]{2,1,0:T(2,128)S(1)} async-done(((f32[512,2,128]{2,1,0:T(2,128)}), f32[512,2,128]{2,1,0:T(2,128)S(1)}, u32[]{:S(2)}, u32[]{:S(2)}) %all-to-all-start.1) | async-done | bytes 524320 | tf_op jit(solution)/shard_map/all_to_all | solution.py:340
  78.4 0.8 gram.1
  79.2 32.2 %all_to_all.26 = f32[512,2,128]{2,1,0:T(2,128)S(1)} all-to-all(f32[512,2,128]{2,1,0:T(2,128)S(1)} %bitcast.20), channel_id=1, replica_groups=mesh['dom'=32,'band'=16] {'band','dom'}, dimensions={0} | all-to-all | bytes 1048576 | tf_op jit(solution)/shard_map/all_to_all | solution.py:340
  111.4 0.1 sum.1
  111.5 32.4 %all_to_all.27 = f32[512,2,128]{2,1,0:T(2,128)S(1)} all-to-all(f32[512,2,128]{2,1,0:T(2,128)S(1)} %bitcast.19), channel_id=1, replica_groups=mesh['dom'=32,'band'=16] {'band','dom'}, dimensions={0} | all-to-all | bytes 1048576 | tf_op jit(solution)/shard_map/all_to_all | solution.py:340
  143.9 25.9 %solve.1 = f32[768,128]{1,0:T(8,128)S(1)} custom-call(s32[1]{0:T(128)} %bitcast.odd, f32[1024,128]{1,0:T(8,128)S(1)} %bitcast.17, f32[1024,128]{1,0:T(8,128)S(1)} %bitcast.14), custom_call_target="tpu_custom_call" | custom-call | tf_op jit(solution)/shard_map/solve/pallas_call | solution.py:320
  169.8 17.0 %all_to_all.28 = f32[16,48,128]{2,1,0:T(8,128)S(1)} all-to-all(f32[16,48,128]{2,1,0:T(8,128)S(1)} %bitcast.22), channel_id=1, replica_groups=mesh['dom'=32,'band'=16] {'band'}, dimensions={0} | all-to-all | bytes 786432 | tf_op jit(solution)/shard_map/all_to_all | solution.py:340
  186.8 0.8 unpack.1
Async XLA Ops:
  0.0 1.0 copy-start.3
  1.0 0.7 copy-start.7
  1.7 33.8 %copy-start.4 = (bf16[192,192]{1,0:T(8,128)(2,1)S(1)}, bf16[192,192]{1,0:T(8,128)(2,1)}, u32[]{:S(2)}) copy-start(bf16[192,192]{1,0:T(8,128)(2,1)} %constant.34.clone.v2) | copy-start | bytes 221188
  1.7 33.8 %copy-start.5 = (bf16[192,192]{1,0:T(8,128)(2,1)S(1)}, bf16[192,192]{1,0:T(8,128)(2,1)}, u32[]{:S(2)}) copy-start(bf16[192,192]{1,0:T(8,128)(2,1)} %constant.33.clone.v1) | copy-start | bytes 221188
  1.7 33.8 %copy-start.6 = (bf16[192,192]{1,0:T(8,128)(2,1)S(1)}, bf16[192,192]{1,0:T(8,128)(2,1)}, u32[]{:S(2)}) copy-start(bf16[192,192]{1,0:T(8,128)(2,1)} %constant.32.clone.v0) | copy-start | bytes 221188
  2.0 33.5 %copy-start = (bf16[512,512]{1,0:T(8,128)(2,1)S(1)}, bf16[512,512]{1,0:T(8,128)(2,1)}, u32[]{:S(2)}) copy-start(bf16[512,512]{1,0:T(8,128)(2,1)} %constant.31.clone.m2) | copy-start | bytes 1572868
  2.1 33.5 %copy-start.1 = (bf16[512,512]{1,0:T(8,128)(2,1)S(1)}, bf16[512,512]{1,0:T(8,128)(2,1)}, u32[]{:S(2)}) copy-start(bf16[512,512]{1,0:T(8,128)(2,1)} %constant.30.clone.m1) | copy-start | bytes 1572868
  2.1 33.5 %copy-start.2 = (bf16[512,512]{1,0:T(8,128)(2,1)S(1)}, bf16[512,512]{1,0:T(8,128)(2,1)}, u32[]{:S(2)}) copy-start(bf16[512,512]{1,0:T(8,128)(2,1)} %constant.29.clone.m0) | copy-start | bytes 1572868
  40.7 37.6 %all-to-all-start.1 = ((f32[512,2,128]{2,1,0:T(2,128)}), f32[512,2,128]{2,1,0:T(2,128)S(1)}, u32[]{:S(2)}, u32[]{:S(2)}) async-start(f32[512,2,128]{2,1,0:T(2,128)} %bitcast.4), calls=%async_computation.1 | async-start | bytes 1048576 | tf_op jit(solution)/shard_map/all_to_all | solution.py:340

commit v2 on v1

v2 whole, which is shorter than its diff:
```python
import jax
import jax.numpy as jnp
import numpy as np
from jax import lax
from jax.experimental import pallas as pl
from jax.experimental.pallas import tpu as pltpu
from jax.sharding import PartitionSpec as P

NB = 512
LX = 32
LY = 16
NZ = 192
CELLS = LX * LY
NPTS = NZ * CELLS
DEG = 4
DOM = 32
BAND = 16
TILE = NB // BAND
DEPTH = NZ // DOM
LANES = 128
ALL = ("band", "dom")

COEF = (
    -5369.0 / 1800.0,
    12.0 / 7.0,
    -15.0 / 56.0,
    10.0 / 189.0,
    -1.0 / 112.0,
    2.0 / 1925.0,
    -1.0 / 16632.0,
)
INV_SPACING2 = 4.0
CENTRE = 24.0
HALF_WIDTH = 20.0

HIGHEST = lax.Precision.HIGHEST
f32 = jnp.float32
bf16 = jnp.bfloat16


def split_constant(matrix):
    pieces = []
    rest = matrix.astype(np.float64)
    for _ in range(2):
        piece = rest.astype(np.float32).astype(bf16)
        pieces.append(piece)
        rest = rest - piece.astype(np.float64)
    return pieces


def plane_matrix():
    out = np.zeros((CELLS, CELLS))
    scale = -0.5 * INV_SPACING2 / HALF_WIDTH
    for y in range(LY):
        for x in range(LX):
            row = y * LX + x
            out[row, row] += scale * 3.0 * COEF[0] - CENTRE / HALF_WIDTH
            for k in range(1, 7):
                for step in (k, -k):
                    out[row, y * LX + (x + step) % LX] += scale * COEF[k]
                    out[row, (y + step) % LY * LX + x] += scale * COEF[k]
    return out


def layer_matrix():
    out = np.zeros((NZ, NZ))
    scale = -0.5 * INV_SPACING2 / HALF_WIDTH
    for k in range(1, 7):
        out += scale * COEF[k] * (np.eye(NZ, k=k) + np.eye(NZ, k=-k))
    return out


def split_value(value):
    high = value.astype(bf16)
    return high, (value - high.astype(f32)).astype(bf16)


def dot_split(left, right):
    def dot(a, b):
        return jnp.dot(a, b, preferred_element_type=f32)

    return (dot(left[0], right[1]) + dot(left[1], right[0])) + dot(left[0], right[0])


def pack_kernel(psi, potential, out):
    for layer in range(DEPTH):
        for quarter in range(4):
            lanes = slice(quarter * LANES, (quarter + 1) * LANES)
            row = layer * 8 + quarter
            out[pl.ds(row, TILE, stride=8 * DEPTH), :] = psi[layer, :, lanes]
            out[pl.ds(row + 4, TILE, stride=8 * DEPTH), :] = jnp.broadcast_to(
                potential[layer : layer + 1, lanes] * (1.0 / HALF_WIDTH), (TILE, LANES)
            )


def filter_kernel(rows, strip, m_layer, out, scratch, m_plane):
    for piece in range(2):
        for i in range(4):
            for j in range(4):
                at = (j - i) % 4 * LANES
                m_plane[piece, i * LANES : (i + 1) * LANES, j * LANES : (j + 1) * LANES] = strip[
                    piece, :, at : at + LANES
                ]
    start = jnp.concatenate([rows[pl.ds(q, NZ, stride=8), :] for q in range(4)], axis=1)
    potential = jnp.concatenate([rows[pl.ds(4 + q, NZ, stride=8), :] for q in range(4)], axis=1)
    plane = (m_plane[0], m_plane[1])
    layers = (m_layer[0], m_layer[1])

    def apply(values):
        pieces = split_value(values)
        return dot_split(pieces, plane) + dot_split(layers, pieces) + potential * values

    previous = start
    current = apply(start)
    for _ in range(1, DEG):
        previous, current = current, 2.0 * apply(current) - previous
    norm = jnp.sum(jnp.sum(current * current, axis=0, keepdims=True), axis=1, keepdims=True) * (
        1.0 / NPTS
    )
    for quarter in range(4):
        scratch[quarter * NZ : (quarter + 1) * NZ, :] = current[
            :, quarter * LANES : (quarter + 1) * LANES
        ]
    lane = lax.broadcasted_iota(jnp.int32, (DOM, LANES), 1)
    norms = jnp.broadcast_to(norm, (DOM, LANES))
    for piece in range(BAND):
        first = scratch[pl.ds((piece % 4) * NZ + piece // 4, DOM, stride=DEPTH), :]
        half = piece // 2
        second = scratch[pl.ds((half % 4) * NZ + 4 + half // 4, DOM, stride=DEPTH), :]
        if piece % 2:
            second = pltpu.roll(second, 64, 1)
        out[pl.ds(piece * 2 * DOM, DOM, stride=2), :] = first
        out[pl.ds(piece * 2 * DOM + 1, DOM, stride=2), :] = jnp.where(lane < 64, second, norms)


def points_of(rows):
    first = rows[pl.ds(0, NB, stride=2), :]
    second = rows[pl.ds(1, NB, stride=2), :]
    lane = lax.broadcasted_iota(jnp.int32, (NB, LANES), 1)
    return first, jnp.where(lane < 64, second, 0.0), second


def dot_nt(a, b):
    return lax.dot_general(
        a, b, (((1,), (1,)), ((), ())), precision=HIGHEST, preferred_element_type=f32
    )


def dot_nn(a, b):
    return jnp.dot(a, b, precision=HIGHEST, preferred_element_type=f32)


def gram_kernel(rows, out):
    first, second, _ = points_of(rows)
    points = jnp.concatenate([first, second], axis=1)
    low, high = points[:256], points[256:]
    row = lax.broadcasted_iota(jnp.int32, (256, 256), 0)
    col = lax.broadcasted_iota(jnp.int32, (256, 256), 1)
    folded = jnp.where(col <= row, dot_nt(low, low), dot_nt(high, high))
    below = dot_nt(high, low)
    out[0:256, :] = folded[:, :LANES]
    out[256:512, :] = folded[:, LANES:]
    out[512:768, :] = below[:, :LANES]
    out[768:1024, :] = below[:, LANES:]


def sum_kernel(parts, out):
    total = jnp.sum(parts[...].reshape(8, 16, 8, LANES), axis=0)
    total = jnp.sum(total, axis=0)
    total = total + pltpu.roll(total, 4, 0)
    total = (total + pltpu.roll(total, 2, 0)) * (1.0 / NPTS)
    out[...] = jnp.broadcast_to(total[None], (NB // 4, 8, LANES)).reshape(2 * NB, LANES)


def invert_block(m, ones):
    full = (8, LANES)
    sub = lax.broadcasted_iota(jnp.int32, full, 0)
    lane = lax.broadcasted_iota(jnp.int32, full, 1)

    def row(value, u):
        return jnp.broadcast_to(value[u : u + 1, :], full)

    def column(value, at):
        return jnp.broadcast_to(value[:, at : at + 1], full)

    for panel in range(16):
        base = 8 * panel
        inside = (lane >= base) & (lane < base + 8)
        v = m[base : base + 8, :]
        a = [column(v, base + t) * ones for t in range(8)]
        v = jnp.where(inside, jnp.where(lane - base == sub, 1.0, 0.0), v)
        v_rows = [row(v, u) for u in range(8)]
        lower = [jnp.zeros(full, f32) for _ in range(7)]
        scale = jnp.zeros(full, f32)
        for k in range(8):
            here = sub == k
            pivots = [row(a[k], j) for j in range(8)]
            root = lax.rsqrt(pivots[k])
            inverse = root * root
            for t in range(k):
                lower[t] = jnp.where(here, a[t], lower[t])
            scale = jnp.where(here, root, scale)
            swept = jnp.where(here, -inverse, a[k] * inverse)
            for j in range(8):
                if j != k:
                    a[j] = jnp.where(here, 0.0, a[j]) - swept * pivots[j]
            a[k] = swept
        done = v
        for t in range(7):
            done = done - lower[t] * v_rows[t]
        m[base : base + 8, :] = jnp.where(lane < base + 8, done * scale, 0.0)
        y = [a[u] * v_rows[u] for u in range(8)]
        y = ((y[0] + y[1]) + (y[2] + y[3])) + ((y[4] + y[5]) + (y[6] + y[7]))
        y_rows = [row(y, u) for u in range(8)]
        for q in range(panel + 1, 16):
            d = m[8 * q : 8 * q + 8, :]
            u = [column(d, base + t) * y_rows[t] for t in range(8)]
            u = ((u[0] + u[1]) + (u[2] + u[3])) + ((u[4] + u[5]) + (u[6] + u[7]))
            m[8 * q : 8 * q + 8, :] = jnp.where(inside, 0.0, d) + u


def solve_kernel(gram, rows, out, s_ref, x_ref, block, ones_ref):
    first, second, raw = points_of(rows)
    x_ref[:, :LANES] = first
    x_ref[:, LANES:] = second
    ones_ref[...] = jnp.ones((8, LANES), f32)
    folded = jnp.concatenate([gram[0:256, :], gram[256:512, :]], axis=1)
    flipped = folded.T
    row = lax.broadcasted_iota(jnp.int32, (256, 256), 0)
    col = lax.broadcasted_iota(jnp.int32, (256, 256), 1)
    low = jnp.where(col <= row, folded, flipped)
    norms = jnp.broadcast_to(raw[256:, LANES - 1 : LANES], (256, 256))
    high = jnp.where(col == row, norms, jnp.where(col > row, folded, flipped))
    s_ref[0, :256, :] = low[:, :LANES]
    s_ref[1, :256, :] = low[:, LANES:]
    s_ref[0, 256:, :] = gram[512:768, :]
    s_ref[1, 256:, :] = gram[768:1024, :]
    s_ref[2, 256:, :] = high[:, :LANES]
    s_ref[3, 256:, :] = high[:, LANES:]

    def step(j, carry):
        at = pl.ds(pl.multiple_of(j * LANES, LANES), LANES)
        block[...] = s_ref[j, at, :]
        invert_block(block, ones_ref[...])
        inverse = block[...]
        x_ref[at, :] = dot_nn(inverse, x_ref[at, :])
        for now in range(3):

            @pl.when(j == now)
            def _():
                here = slice(now * LANES, (now + 1) * LANES)
                rest = slice((now + 1) * LANES, NB)
                panel = dot_nt(s_ref[now, rest, :], inverse)
                x_ref[rest, :] = x_ref[rest, :] - dot_nn(panel, x_ref[here, :])
                for k in range(now + 1, 4):
                    skip = (k - now - 1) * LANES
                    s_ref[k, k * LANES :, :] = s_ref[k, k * LANES :, :] - dot_nt(
                        panel[skip:], panel[skip : skip + LANES]
                    )

        return carry

    lax.fori_loop(0, 4, step, 0)
    for tile in range(BAND):
        at = tile * TILE
        out[tile * 48 : tile * 48 + 32, :] = x_ref[at : at + TILE, :LANES]
        out[tile * 48 + 32 : tile * 48 + 48, :] = x_ref[at : at + 16, LANES:] + pltpu.roll(
            x_ref[at + 16 : at + 32, LANES:], 64, 1
        )


def unpack_kernel(rows, out):
    for piece in range(BAND):
        quarter = piece % 4
        out[piece // 4, :, quarter * LANES : (quarter + 1) * LANES] = rows[
            piece * 48 : piece * 48 + 32, :
        ]
    lower = lax.broadcasted_iota(jnp.int32, (16, LANES), 1) < 64
    for half in range(8):
        lanes = slice((half % 4) * LANES, (half % 4 + 1) * LANES)
        even = rows[2 * half * 48 + 32 : 2 * half * 48 + 48, :]
        odd = rows[(2 * half + 1) * 48 + 32 : (2 * half + 1) * 48 + 48, :]
        out[4 + half // 4, 0:16, lanes] = jnp.where(lower, even, pltpu.roll(odd, 64, 1))
        out[4 + half // 4, 16:32, lanes] = jnp.where(lower, pltpu.roll(even, 64, 1), odd)


def whole():
    return pl.BlockSpec(memory_space=pltpu.VMEM)


def call(kernel, name, shape, specs, scratch=()):
    return pl.pallas_call(
        kernel,
        name=name,
        out_shape=jax.ShapeDtypeStruct(shape, f32),
        in_specs=specs,
        out_specs=whole(),
        scratch_shapes=list(scratch),
        compiler_params=pltpu.CompilerParams(vmem_limit_bytes=48 << 20),
    )


def do_pack(psi, potential):
    return call(pack_kernel, "pack", (TILE * 8 * DEPTH, LANES), [whole()] * 2)(psi, potential)


def do_filter(rows):
    strip = np.stack(split_constant(plane_matrix()[:LANES]))
    layers = np.stack(split_constant(layer_matrix()))
    return call(
        filter_kernel,
        "filter",
        (2 * NB, LANES),
        [whole()] * 3,
        [pltpu.VMEM((4 * NZ, LANES), f32), pltpu.VMEM((2, CELLS, CELLS), bf16)],
    )(rows, jnp.asarray(strip), jnp.asarray(layers))


def do_gram(rows):
    return call(gram_kernel, "gram", (2 * NB, LANES), [whole()])(rows)


def do_sum(parts):
    return call(sum_kernel, "sum", (2 * NB, LANES), [whole()])(parts)


def do_solve(gram, rows):
    return call(
        solve_kernel,
        "solve",
        (BAND * 48, LANES),
        [whole(), whole()],
        [
            pltpu.VMEM((4, NB, LANES), f32),
            pltpu.VMEM((NB, 2 * LANES), f32),
            pltpu.VMEM((LANES, LANES), f32),
            pltpu.VMEM((8, LANES), f32),
        ],
    )(gram, rows)


def do_unpack(rows):
    return call(unpack_kernel, "unpack", (DEPTH, TILE, CELLS), [whole()])(rows)


def exchange(rows, axis, parts):
    shaped = rows.reshape(parts, rows.shape[0] // parts, LANES)
    return lax.all_to_all(shaped, axis, 0, 0).reshape(rows.shape)


def shards(psi, potential):
    bands = exchange(do_pack(jnp.transpose(psi, (1, 0, 2)), potential), "dom", DOM)
    points = exchange(do_filter(bands), ALL, NB)
    parts = exchange(do_gram(points), ALL, NB)
    gram = exchange(do_sum(parts), ALL, NB)
    result = exchange(do_solve(gram, points), "band", BAND)
    return jnp.transpose(do_unpack(result), (1, 0, 2))


def solution(mesh):
    placed = (P("band", "dom", None), P("dom", None))
    return jax.shard_map(
        shards, mesh=mesh, in_specs=placed, out_specs=P("band", "dom", None), check_vma=False
    )
```

time: 190 us -> 182 us (0.958)
  blocking collectives: 115 us -> 152 us
  waiting for transfers between devices: 21.7 us -> 0 us
  starting transfers between devices: 15.9 us -> 0 us
  Pallas kernels: 33.1 us -> 26.2 us
    all_to_all x4 -> x5, blocking collectives: 115 us -> 152 us  [exchange(): return lax.all_to_all(shaped, axis, 0, 0).reshape(rows.shape)]
    all_to_all x1 -> x0, waiting for transfers between devices: 21.7 us -> none  [exchange(): return lax.all_to_all(shaped, axis, 0, 0).reshape(rows.shape)]
    all_to_all x1 -> x0, starting transfers between devices: 15.9 us -> none  [exchange(): return lax.all_to_all(shaped, axis, 0, 0).reshape(rows.shape)]
    pallas_call x3, Pallas kernels: 31.9 us -> 24.9 us  [the longest x1 21.5 us: do_solve(): call(solve_kernel, 'solve', (BAND * 48, LANES), [whole(), whole()], [pltp...]
  transfers between devices with their start and end apart: 1 -> 0, of which waited for: 1 -> 0; matrix products, arithmetic and copies ran while one was open for 0% -> 0% of each run, Pallas kernels for 0% -> 0%
where the time goes in v2:
time: 182 us; the launch traced here: 180 us
  blocking collectives  152 us (84%)
  Pallas kernels  26.2 us (14%)
    all_to_all x5, blocking collectives, exchange(): return lax.all_to_all(shaped, axis, 0, 0).reshape(rows.shape)  152 us
    pallas_call x1, Pallas kernels, do_solve(): call(solve_kernel, 'solve', (BAND * 48, LANES), [whole(), whole()], [pltp...  21.5 us

profile of v2, /device:TPU:6, one launch (start us, length us, event | category | flops | bytes accessed | tf_op | source)
XLA Modules:
  0.0 180.3 jit_solution(11470405957203002104)
XLA Ops:
  0.0 0.0 copy-start
  0.0 1.0 copy-done
  1.0 0.0 copy-start.3
  1.0 0.7 copy-done.3
  1.7 0.3 pack.1
  2.0 0.0 copy-start.1
  2.1 0.0 copy-start.2
  2.1 33.4 %all_to_all.25 = f32[32,48,128]{2,1,0:T(8,128)S(1)} all-to-all(f32[32,48,128]{2,1,0:T(8,128)S(1)} %bitcast.15), channel_id=1, replica_groups=mesh['dom'=32,'band'=16] {'dom'}, dimensions={0} | all-to-all | bytes 1572864 | tf_op jit(solution)/shard_map/all_to_all | solution.py:348
  35.5 0.0 copy-done.1
  35.5 0.0 copy-done.2
  35.5 2.6 %filter.1 = f32[1024,128]{1,0:T(8,128)S(1)} custom-call(f32[1536,128]{1,0:T(8,128)S(1)} %bitcast.14, bf16[2,128,512]{2,1,0:T(8,128)(2,1)S(1)} %copy-done.1, bf16[2,192,192]{2,1,0:T(8,128)(2,1)S(1)} %copy-done.2), custom_call_target="tpu_custom_call" | custom-call | tf_op jit(solution)/shard_map/filter/pallas_call | solution.py:310
  38.1 37.5 %all_to_all.26 = f32[512,2,128]{2,1,0:T(2,128)S(1)} all-to-all(f32[512,2,128]{2,1,0:T(2,128)S(1)} %bitcast.16), channel_id=1, replica_groups=mesh['dom'=32,'band'=16] {'band','dom'}, dimensions={0} | all-to-all | bytes 1048576 | tf_op jit(solution)/shard_map/all_to_all | solution.py:348
  75.6 0.8 gram.1
  76.4 32.2 %all_to_all.27 = f32[512,2,128]{2,1,0:T(2,128)S(1)} all-to-all(f32[512,2,128]{2,1,0:T(2,128)S(1)} %bitcast.19), channel_id=1, replica_groups=mesh['dom'=32,'band'=16] {'band','dom'}, dimensions={0} | all-to-all | bytes 1048576 | tf_op jit(solution)/shard_map/all_to_all | solution.py:348
  108.6 0.1 sum.1
  108.7 32.2 %all_to_all.28 = f32[512,2,128]{2,1,0:T(2,128)S(1)} all-to-all(f32[512,2,128]{2,1,0:T(2,128)S(1)} %bitcast.18), channel_id=1, replica_groups=mesh['dom'=32,'band'=16] {'band','dom'}, dimensions={0} | all-to-all | bytes 1048576 | tf_op jit(solution)/shard_map/all_to_all | solution.py:348
  140.9 21.5 %solve.1 = f32[768,128]{1,0:T(8,128)S(1)} custom-call(f32[1024,128]{1,0:T(8,128)S(1)} %bitcast.20, f32[1024,128]{1,0:T(8,128)S(1)} %bitcast.13), custom_call_target="tpu_custom_call" | custom-call | tf_op jit(solution)/shard_map/solve/pallas_call | solution.py:328
  162.4 17.0 %all_to_all.29 = f32[16,48,128]{2,1,0:T(8,128)S(1)} all-to-all(f32[16,48,128]{2,1,0:T(8,128)S(1)} %bitcast.22), channel_id=1, replica_groups=mesh['dom'=32,'band'=16] {'band'}, dimensions={0} | all-to-all | bytes 786432 | tf_op jit(solution)/shard_map/all_to_all | solution.py:348
  179.4 0.8 unpack.1
Async XLA Ops:
  0.0 1.0 copy-start
  1.0 0.7 copy-start.3
  2.0 33.5 %copy-start.1 = (bf16[2,128,512]{2,1,0:T(8,128)(2,1)S(1)}, bf16[2,128,512]{2,1,0:T(8,128)(2,1)}, u32[]{:S(2)}) copy-start(bf16[2,128,512]{2,1,0:T(8,128)(2,1)} %constant.4.clone.strip) | copy-start | bytes 786436
  2.1 33.5 %copy-start.2 = (bf16[2,192,192]{2,1,0:T(8,128)(2,1)S(1)}, bf16[2,192,192]{2,1,0:T(8,128)(2,1)}, u32[]{:S(2)}) copy-start(bf16[2,192,192]{2,1,0:T(8,128)(2,1)} %constant.5.clone.m_layer) | copy-start | bytes 442372

commit v3 on v2

--- a/solution.py
+++ b/solution.py
@@ -4,7 +4,7 @@
 from jax import lax
 from jax.experimental import pallas as pl
 from jax.experimental.pallas import tpu as pltpu
-from jax.sharding import PartitionSpec as P
+from jax.sharding import Mesh, PartitionSpec as P
 
 NB = 512
 LX = 32
@@ -18,7 +18,13 @@
 TILE = NB // BAND
 DEPTH = NZ // DOM
 LANES = 128
-ALL = ("band", "dom")
+SIDES = (8, 2, 2, 8, 2)
+NAMES = ("y", "xh", "core", "z", "xl")
+LAYERS = ("y", "xh", "core")
+BANDS = ("z", "xl")
+ALL = BANDS + LAYERS
+PLANE = ("y", "xh", "xl")
+IN_PLANE = 32
 
 COEF = (
     -5369.0 / 1800.0,
@@ -150,7 +156,7 @@
     return jnp.dot(a, b, precision=HIGHEST, preferred_element_type=f32)
 
 
-def gram_kernel(rows, out):
+def gram_kernel(core, rows, keep, send):
     first, second, _ = points_of(rows)
     points = jnp.concatenate([first, second], axis=1)
     low, high = points[:256], points[256:]
@@ -158,18 +164,20 @@
     col = lax.broadcasted_iota(jnp.int32, (256, 256), 1)
     folded = jnp.where(col <= row, dot_nt(low, low), dot_nt(high, high))
     below = dot_nt(high, low)
-    out[0:256, :] = folded[:, :LANES]
-    out[256:512, :] = folded[:, LANES:]
-    out[512:768, :] = below[:, :LANES]
-    out[768:1024, :] = below[:, LANES:]
-
-
-def sum_kernel(parts, out):
-    total = jnp.sum(parts[...].reshape(8, 16, 8, LANES), axis=0)
-    total = jnp.sum(total, axis=0)
-    total = total + pltpu.roll(total, 4, 0)
-    total = (total + pltpu.roll(total, 2, 0)) * (1.0 / NPTS)
-    out[...] = jnp.broadcast_to(total[None], (NB // 4, 8, LANES)).reshape(2 * NB, LANES)
+    first = core[0] == 0
+    for half in range(2):
+        lanes = slice(half * LANES, (half + 1) * LANES)
+        at = slice(half * 256, (half + 1) * 256)
+        keep[at, :] = jnp.where(first, folded[:, lanes], below[:, lanes])
+        send[at, :] = jnp.where(first, below[:, lanes], folded[:, lanes])
+
+
+def sum_kernel(scale):
+    def kernel(parts, out):
+        total = jnp.sum(parts[...], axis=0) * scale
+        out[...] = jnp.broadcast_to(total[None], out.shape)
+
+    return kernel
 
 
 def invert_block(m, ones):
@@ -219,12 +227,14 @@
             m[8 * q : 8 * q + 8, :] = jnp.where(inside, 0.0, d) + u
 
 
-def solve_kernel(gram, rows, out, s_ref, x_ref, block, ones_ref):
+def solve_kernel(core, mine, other, rows, out, s_ref, x_ref, block, ones_ref):
     first, second, raw = points_of(rows)
     x_ref[:, :LANES] = first
     x_ref[:, LANES:] = second
     ones_ref[...] = jnp.ones((8, LANES), f32)
-    folded = jnp.concatenate([gram[0:256, :], gram[256:512, :]], axis=1)
+    swap = core[0] == 0
+    folded = jnp.where(swap, mine[...], other[...])
+    folded = jnp.concatenate([folded[:256], folded[256:]], axis=1)
     flipped = folded.T
     row = lax.broadcasted_iota(jnp.int32, (256, 256), 0)
     col = lax.broadcasted_iota(jnp.int32, (256, 256), 1)
@@ -233,8 +243,8 @@
     high = jnp.where(col == row, norms, jnp.where(col > row, folded, flipped))
     s_ref[0, :256, :] = low[:, :LANES]
     s_ref[1, :256, :] = low[:, LANES:]
-    s_ref[0, 256:, :] = gram[512:768, :]
-    s_ref[1, 256:, :] = gram[768:1024, :]
+    s_ref[0, 256:, :] = jnp.where(swap, other[:256, :], mine[:256, :])
+    s_ref[1, 256:, :] = jnp.where(swap, other[256:, :], mine[256:, :])
     s_ref[2, 256:, :] = high[:, :LANES]
     s_ref[3, 256:, :] = high[:, LANES:]
 
@@ -288,6 +298,10 @@
     return pl.BlockSpec(memory_space=pltpu.VMEM)
 
 
+def scalar():
+    return pl.BlockSpec(memory_space=pltpu.SMEM)
+
+
 def call(kernel, name, shape, specs, scratch=()):
     return pl.pallas_call(
         kernel,
@@ -316,27 +330,35 @@
     )(rows, jnp.asarray(strip), jnp.asarray(layers))
 
 
-def do_gram(rows):
-    return call(gram_kernel, "gram", (2 * NB, LANES), [whole()])(rows)
-
-
-def do_sum(parts):
-    return call(sum_kernel, "sum", (2 * NB, LANES), [whole()])(parts)
-
-
-def do_solve(gram, rows):
+def do_gram(core, rows):
+    half = jax.ShapeDtypeStruct((NB, LANES), f32)
+    return pl.pallas_call(
+        gram_kernel,
+        name="gram",
+        out_shape=(half, half),
+        in_specs=[scalar(), whole()],
+        out_specs=(whole(), whole()),
+        compiler_params=pltpu.CompilerParams(vmem_limit_bytes=48 << 20),
+    )(core, rows)
+
+
+def do_sum(parts, copies, scale):
+    return call(sum_kernel(scale), "sum", (copies,) + parts.shape[1:], [whole()])(parts)
+
+
+def do_solve(core, mine, other, rows):
     return call(
         solve_kernel,
         "solve",
         (BAND * 48, LANES),
-        [whole(), whole()],
+        [scalar(), whole(), whole(), whole()],
         [
             pltpu.VMEM((4, NB, LANES), f32),
             pltpu.VMEM((NB, 2 * LANES), f32),
             pltpu.VMEM((LANES, LANES), f32),
             pltpu.VMEM((8, LANES), f32),
         ],
-    )(gram, rows)
+    )(core, mine, other, rows)
 
 
 def do_unpack(rows):
@@ -348,17 +370,31 @@
     return lax.all_to_all(shaped, axis, 0, 0).reshape(rows.shape)
 
 
+def swap_cores(value):
+    return lax.ppermute(value, "core", [(0, 1), (1, 0)])
+
+
+def gram_sum(keep, send):
+    depth = SIDES[3]
+    half = (keep + swap_cores(send)).reshape(IN_PLANE, NB // IN_PLANE, LANES)
+    half = do_sum(lax.all_to_all(half, PLANE, 0, 0), depth, 1.0)
+    half = do_sum(lax.all_to_all(half, "z", 0, 0), IN_PLANE, 1.0 / NPTS)
+    return lax.all_to_all(half, PLANE, 0, 0).reshape(NB, LANES)
+
+
 def shards(psi, potential):
-    bands = exchange(do_pack(jnp.transpose(psi, (1, 0, 2)), potential), "dom", DOM)
+    core = lax.axis_index("core").astype(jnp.int32).reshape(1)
+    psi, core = lax.optimization_barrier((psi, core))
+    bands = exchange(do_pack(jnp.transpose(psi, (1, 0, 2)), potential), LAYERS, DOM)
     points = exchange(do_filter(bands), ALL, NB)
-    parts = exchange(do_gram(points), ALL, NB)
-    gram = exchange(do_sum(parts), ALL, NB)
-    result = exchange(do_solve(gram, points), "band", BAND)
+    gram = gram_sum(*do_gram(core, points))
+    result = exchange(do_solve(core, gram, swap_cores(gram), points), BANDS, BAND)
     return jnp.transpose(do_unpack(result), (1, 0, 2))
 
 
 def solution(mesh):
-    placed = (P("band", "dom", None), P("dom", None))
+    split = Mesh(np.asarray(mesh.devices).reshape(SIDES), NAMES)
+    bands = P(BANDS, LAYERS, None)
     return jax.shard_map(
-        shards, mesh=mesh, in_specs=placed, out_specs=P("band", "dom", None), check_vma=False
+        shards, mesh=split, in_specs=(bands, P(LAYERS, None)), out_specs=bands, check_vma=False
     )

time: 182 us -> 169 us (0.929)
  blocking collectives: 152 us -> 132 us
  starting transfers between devices: 0 us -> 4.01 us
  waiting for transfers between devices: 0 us -> 2.82 us
    all_to_all x5 -> x3, blocking collectives: 152 us -> 88.5 us  [exchange(): return lax.all_to_all(shaped, axis, 0, 0).reshape(rows.shape)]
    all_to_all x0 -> x3, blocking collectives: none -> 43.1 us  [the longest x1 16.3 us: gram_sum(): half = do_sum(lax.all_to_all(half, PLANE, 0, 0), depth, 1.0)]
    ppermute x0 -> x2, starting transfers between devices: none -> 4.01 us  [swap_cores(): return lax.ppermute(value, 'core', [(0, 1), (1, 0)])]
    ppermute x0 -> x2, waiting for transfers between devices: none -> 2.82 us  [swap_cores(): return lax.ppermute(value, 'core', [(0, 1), (1, 0)])]
    pallas_call x3 -> x4, Pallas kernels: 22.4 us -> 22.4 us  [the longest x1 21.5 us: do_solve(): call(solve_kernel, 'solve', (BAND * 48, LANES), [scalar(), whole(), whole...]
  transfers between devices with their start and end apart: 0 -> 2, of which waited for: 0 -> 2; matrix products, arithmetic and copies ran while one was open for 0% -> 0% of each run, Pallas kernels for 0% -> 0%
where the time goes in v3:
time: 169 us; the launch traced here: 166 us
  blocking collectives  132 us (78%)
  Pallas kernels  26.2 us (16%)
  starting transfers between devices  4.01 us (2%)
  waiting for transfers between devices  2.82 us (2%)
  local copies, waits for them, and re-layouts  1.73 us (1%)
    all_to_all x3, blocking collectives, exchange(): return lax.all_to_all(shaped, axis, 0, 0).reshape(rows.shape)  88.5 us
    pallas_call x1, Pallas kernels, do_solve(): call(solve_kernel, 'solve', (BAND * 48, LANES), [scalar(), whole(), whole...  21.5 us
    all_to_all x1, blocking collectives, gram_sum(): half = do_sum(lax.all_to_all(half, PLANE, 0, 0), depth, 1.0)  16.3 us
    all_to_all x1, blocking collectives, gram_sum(): return lax.all_to_all(half, PLANE, 0, 0).reshape(NB, LANES)  15.2 us
    all_to_all x1, blocking collectives, gram_sum(): half = do_sum(lax.all_to_all(half, 'z', 0, 0), IN_PLANE, 1.0 / NPTS)  11.5 us
    ppermute x2, starting transfers between devices, swap_cores(): return lax.ppermute(value, 'core', [(0, 1), (1, 0)])  4.01 us
  transfers between devices with their start and end apart: 2, of which 2 were waited for; matrix products, arithmetic and copies ran while one was open for 0% of the time, Pallas kernels for 0%

profile of v3, /device:TPU:6, one launch (start us, length us, event | category | flops | bytes accessed | tf_op | source)
XLA Modules:
  0.0 166.4 jit_solution(1560174503132339280)
XLA Ops:
  0.0 0.0 copy-start
  0.0 1.0 copy-done
  1.0 0.0 copy-start.3
  1.0 0.7 copy-done.3
  1.7 0.3 pack.1
  2.0 0.0 copy-start.1
  2.1 0.0 copy-start.2
  2.1 33.4 %all_to_all.30 = f32[32,48,128]{2,1,0:T(8,128)S(1)} all-to-all(f32[32,48,128]{2,1,0:T(8,128)S(1)} %bitcast.14), channel_id=1, replica_groups=mesh['y'=8,'xh'=2,'core'=2,'z'=8,'xl'=2] {'y','xh','core'}, dimensions={0} | all-to-all | bytes 1572864 | tf_op jit(solution)/shard_map/all_to_all | solution.py:370
  35.5 0.0 copy-done.1
  35.5 0.0 copy-done.2
  35.5 2.6 %filter.1 = f32[1024,128]{1,0:T(8,128)S(1)} custom-call(f32[1536,128]{1,0:T(8,128)S(1)} %bitcast.13, bf16[2,128,512]{2,1,0:T(8,128)(2,1)S(1)} %copy-done.1, bf16[2,192,192]{2,1,0:T(8,128)(2,1)S(1)} %copy-done.2), custom_call_target="tpu_custom_call" | custom-call | tf_op jit(solution)/shard_map/filter/pallas_call | solution.py:324
  38.1 37.4 %all_to_all.31 = f32[512,2,128]{2,1,0:T(2,128)S(1)} all-to-all(f32[512,2,128]{2,1,0:T(2,128)S(1)} %bitcast.15), channel_id=1, replica_groups=mesh['y'=8,'xh'=2,'core'=2,'z'=8,'xl'=2] {'z','xl','y','xh','core'}, dimensions={0} | all-to-all | bytes 1048576 | tf_op jit(solution)/shard_map/all_to_all | solution.py:370
  75.6 0.8 gram.1
  76.4 1.9 %collective-permute-start = (f32[512,128]{1,0:T(8,128)S(1)}, f32[512,128]{1,0:T(8,128)S(1)}, u32[]{:S(2)}, u32[]{:S(2)}) collective-permute-start(f32[512,128]{1,0:T(8,128)S(1)} %get-tuple-element.12), channel_id=1, source_target_pairs={{0,16},{16,0},{1,17},{17,1},{2,18},{18,2},{3,19},{19,3},{4,20},{20... | collective-permute-start | bytes 786440 | tf_op jit(solution)/shard_map/ppermute | solution.py:374
  78.3 1.5 collective-permute-done
  79.9 16.3 %all_to_all.32.parts = f32[32,16,128]{2,1,0:T(8,128)S(1)} all-to-all(f32[32,16,128]{2,1,0:T(8,128)S(1)} %bitcast.21), channel_id=1, replica_groups=mesh['y'=8,'xh'=2,'core'=2,'z'=8,'xl'=2] {'y','xh','xl'}, dimensions={0} | all-to-all | bytes 524288 | tf_op jit(solution)/shard_map/all_to_all | solution.py:380
  96.2 11.5 %all_to_all.33.parts = f32[8,16,128]{2,1,0:T(8,128)S(1)} all-to-all(f32[8,16,128]{2,1,0:T(8,128)S(1)} %sum.2), channel_id=1, replica_groups=mesh['y'=8,'xh'=2,'core'=2,'z'=8,'xl'=2] {'z'}, dimensions={0} | all-to-all | bytes 131072 | tf_op jit(solution)/shard_map/all_to_all | solution.py:381
  107.8 15.2 %all_to_all.34 = f32[32,16,128]{2,1,0:T(8,128)S(1)} all-to-all(f32[32,16,128]{2,1,0:T(8,128)S(1)} %sum.3), channel_id=1, replica_groups=mesh['y'=8,'xh'=2,'core'=2,'z'=8,'xl'=2] {'y','xh','xl'}, dimensions={0} | all-to-all | bytes 524288 | tf_op jit(solution)/shard_map/all_to_all | solution.py:382
  123.0 2.1 %collective-permute-start.1 = (f32[512,128]{1,0:T(8,128)S(1)}, f32[512,128]{1,0:T(8,128)S(1)}, u32[]{:S(2)}, u32[]{:S(2)}) collective-permute-start(f32[512,128]{1,0:T(8,128)S(1)} %bitcast.18), channel_id=1, source_target_pairs={{0,16},{16,0},{1,17},{17,1},{2,18},{18,2},{3,19},{19,3},{4,20},{20... | collective-permute-start | bytes 786440 | tf_op jit(solution)/shard_map/ppermute | solution.py:374
  125.1 1.3 collective-permute-done.1.other
  126.4 21.5 %solve.1 = f32[768,128]{1,0:T(8,128)S(1)} custom-call(s32[1]{0:T(128)} %bitcast.core, f32[512,128]{1,0:T(8,128)S(1)} %bitcast.19, f32[512,128]{1,0:T(8,128)S(1)} %collective-permute-done.1.other, f32[1024,128]{1,0:T(8,128)S(1)} %bitcast.12), custom_call_target="tpu_custom_call" | custom-call | tf_op jit(solution)/shard_map/solve/pallas_call | solution.py:350
  148.0 17.6 %all_to_all.35 = f32[16,48,128]{2,1,0:T(8,128)S(1)} all-to-all(f32[16,48,128]{2,1,0:T(8,128)S(1)} %bitcast.17), channel_id=1, replica_groups=mesh['y'=8,'xh'=2,'core'=2,'z'=8,'xl'=2] {'z','xl'}, dimensions={0} | all-to-all | bytes 786432 | tf_op jit(solution)/shard_map/all_to_all | solution.py:370
  165.6 0.8 unpack.1
  (3 shorter events, 0.1 us)
Async XLA Ops:
  0.0 1.0 copy-start
  1.0 0.7 copy-start.3
  2.0 33.5 %copy-start.1 = (bf16[2,128,512]{2,1,0:T(8,128)(2,1)S(1)}, bf16[2,128,512]{2,1,0:T(8,128)(2,1)}, u32[]{:S(2)}) copy-start(bf16[2,128,512]{2,1,0:T(8,128)(2,1)} %constant.10.clone.strip) | copy-start | bytes 786436
  2.1 33.5 %copy-start.2 = (bf16[2,192,192]{2,1,0:T(8,128)(2,1)S(1)}, bf16[2,192,192]{2,1,0:T(8,128)(2,1)}, u32[]{:S(2)}) copy-start(bf16[2,192,192]{2,1,0:T(8,128)(2,1)} %constant.11.clone.m_layer) | copy-start | bytes 442372
  76.4 3.4 %collective-permute-start = (f32[512,128]{1,0:T(8,128)S(1)}, f32[512,128]{1,0:T(8,128)S(1)}, u32[]{:S(2)}, u32[]{:S(2)}) collective-permute-start(f32[512,128]{1,0:T(8,128)S(1)} %get-tuple-element.12), channel_id=1, source_target_pairs={{0,16},{16,0},{1,17},{17,1},{2,18},{18,2},{3,19},{19,3},{4,20},{20... | collective-permute-start | bytes 786440 | tf_op jit(solution)/shard_map/ppermute | solution.py:374
  123.0 3.4 %collective-permute-start.1 = (f32[512,128]{1,0:T(8,128)S(1)}, f32[512,128]{1,0:T(8,128)S(1)}, u32[]{:S(2)}, u32[]{:S(2)}) collective-permute-start(f32[512,128]{1,0:T(8,128)S(1)} %bitcast.18), channel_id=1, source_target_pairs={{0,16},{16,0},{1,17},{17,1},{2,18},{18,2},{3,19},{19,3},{4,20},{20... | collective-permute-start | bytes 786440 | tf_op jit(solution)/shard_map/ppermute | solution.py:374

commit v4 on v3

--- a/solution.py
+++ b/solution.py
@@ -152,10 +152,6 @@
     )
 
 
-def dot_nn(a, b):
-    return jnp.dot(a, b, precision=HIGHEST, preferred_element_type=f32)
-
-
 def gram_kernel(core, rows, keep, send):
     first, second, _ = points_of(rows)
     points = jnp.concatenate([first, second], axis=1)
@@ -180,7 +176,7 @@
     return kernel
 
 
-def invert_block(m, ones):
+def invert_block(m, ones, work):
     full = (8, LANES)
     sub = lax.broadcasted_iota(jnp.int32, full, 0)
     lane = lax.broadcasted_iota(jnp.int32, full, 1)
@@ -191,43 +187,56 @@
     def column(value, at):
         return jnp.broadcast_to(value[:, at : at + 1], full)
 
+    def total(terms):
+        return ((terms[0] + terms[1]) + (terms[2] + terms[3])) + (
+            (terms[4] + terms[5]) + (terms[6] + terms[7])
+        )
+
+    v = m[0:8, :]
     for panel in range(16):
         base = 8 * panel
         inside = (lane >= base) & (lane < base + 8)
-        v = m[base : base + 8, :]
         a = [column(v, base + t) * ones for t in range(8)]
         v = jnp.where(inside, jnp.where(lane - base == sub, 1.0, 0.0), v)
         v_rows = [row(v, u) for u in range(8)]
         lower = [jnp.zeros(full, f32) for _ in range(7)]
         scale = jnp.zeros(full, f32)
+        pivots = [row(a[0], j) for j in range(8)]
         for k in range(8):
             here = sub == k
-            pivots = [row(a[k], j) for j in range(8)]
-            root = lax.rsqrt(pivots[k])
+            ahead = [row(a[k], j) for j in range(k)] + pivots[k:]
+            root = lax.rsqrt(ahead[k])
             inverse = root * root
+            if k < 7:
+                pivots = [None] * (k + 1) + [
+                    row(a[k + 1], j) - (ahead[k + 1] * ahead[j]) * inverse for j in range(k + 1, 8)
+                ]
             for t in range(k):
                 lower[t] = jnp.where(here, a[t], lower[t])
             scale = jnp.where(here, root, scale)
             swept = jnp.where(here, -inverse, a[k] * inverse)
             for j in range(8):
                 if j != k:
-                    a[j] = jnp.where(here, 0.0, a[j]) - swept * pivots[j]
+                    a[j] = jnp.where(here, 0.0, a[j]) - swept * ahead[j]
             a[k] = swept
+        y = total([a[u] * v_rows[u] for u in range(8)])
+        y_rows = [row(y, u) for u in range(8)]
         done = v
         for t in range(7):
             done = done - lower[t] * v_rows[t]
         m[base : base + 8, :] = jnp.where(lane < base + 8, done * scale, 0.0)
-        y = [a[u] * v_rows[u] for u in range(8)]
-        y = ((y[0] + y[1]) + (y[2] + y[3])) + ((y[4] + y[5]) + (y[6] + y[7]))
-        y_rows = [row(y, u) for u in range(8)]
         for q in range(panel + 1, 16):
             d = m[8 * q : 8 * q + 8, :]
-            u = [column(d, base + t) * y_rows[t] for t in range(8)]
-            u = ((u[0] + u[1]) + (u[2] + u[3])) + ((u[4] + u[5]) + (u[6] + u[7]))
-            m[8 * q : 8 * q + 8, :] = jnp.where(inside, 0.0, d) + u
-
-
-def solve_kernel(core, mine, other, rows, out, s_ref, x_ref, block, ones_ref):
+            d = jnp.where(inside, 0.0, d) + total([column(d, base + t) * y_rows[t] for t in range(8)])
+            if q == panel + 1:
+                v = d
+            else:
+                m[8 * q : 8 * q + 8, :] = d
+        for _ in range(-(-len(work) // (16 - panel))):
+            work.pop(0)()
+
+
+def solve_kernel(core, mine, other, rows, out, s_ref, x_ref, blocks, panels, inverses, ones_ref):
     first, second, raw = points_of(rows)
     x_ref[:, :LANES] = first
     x_ref[:, LANES:] = second
@@ -248,34 +257,67 @@
     s_ref[2, 256:, :] = high[:, :LANES]
     s_ref[3, 256:, :] = high[:, LANES:]
 
-    def step(j, carry):
-        at = pl.ds(pl.multiple_of(j * LANES, LANES), LANES)
-        block[...] = s_ref[j, at, :]
-        invert_block(block, ones_ref[...])
-        inverse = block[...]
-        x_ref[at, :] = dot_nn(inverse, x_ref[at, :])
-        for now in range(3):
-
-            @pl.when(j == now)
-            def _():
-                here = slice(now * LANES, (now + 1) * LANES)
-                rest = slice((now + 1) * LANES, NB)
-                panel = dot_nt(s_ref[now, rest, :], inverse)
-                x_ref[rest, :] = x_ref[rest, :] - dot_nn(panel, x_ref[here, :])
-                for k in range(now + 1, 4):
-                    skip = (k - now - 1) * LANES
-                    s_ref[k, k * LANES :, :] = s_ref[k, k * LANES :, :] - dot_nt(
-                        panel[skip:], panel[skip : skip + LANES]
-                    )
-
-        return carry
-
-    lax.fori_loop(0, 4, step, 0)
+    def at(i):
+        return slice(i * LANES, (i + 1) * LANES)
+
+    def split_dot(left, right, dims):
+        def dot(a, b):
+            return lax.dot_general(a, b, (dims, ((), ())), preferred_element_type=f32)
+
+        return (dot(left[0], right[1]) + dot(left[1], right[0])) + dot(left[0], right[0])
+
+    nt, nn = ((1,), (1,)), ((1,), (0,))
+
+    def pieces(ref, i):
+        return ref[i, 0], ref[i, 1]
+
+    def put(ref, i, value):
+        ref[i, 0], ref[i, 1] = split_value(value)
+
+    def form_panel(j, i):
+        put(panels, i, split_dot(split_value(s_ref[j, at(i), :]), pieces(inverses, j), nt))
+
+    def update_s(k, i):
+        s_ref[k, at(i), :] = s_ref[k, at(i), :] - split_dot(
+            pieces(panels, i), pieces(panels, k), nt
+        )
+
+    def solve_x(j):
+        x_ref[at(j), :] = split_dot(pieces(inverses, j), split_value(x_ref[at(j), :]), nn)
+
+    def update_x(j, i):
+        x_ref[at(i), :] = x_ref[at(i), :] - split_dot(
+            pieces(panels, i), split_value(x_ref[at(j), :]), nn
+        )
+
+    ones = ones_ref[...]
+    work = []
+    blocks[0] = s_ref[0, at(0), :]
+    for j in range(4):
+        invert_block(blocks.at[j], ones, work)
+        put(inverses, j, blocks[j])
+        work = []
+        if j < 3:
+            form_panel(j, j + 1)
+            blocks[j + 1] = s_ref[j + 1, at(j + 1), :] - split_dot(
+                pieces(panels, j + 1), pieces(panels, j + 1), nt
+            )
+            for i in range(j + 2, 4):
+                work.append(lambda j=j, i=i: form_panel(j, i))
+                work.append(lambda k=j + 1, i=i: update_s(k, i))
+            for k in range(j + 2, 4):
+                for i in range(k, 4):
+                    work.append(lambda k=k, i=i: update_s(k, i))
+        work.append(lambda j=j: solve_x(j))
+        for i in range(j + 1, 4):
+            work.append(lambda j=j, i=i: update_x(j, i))
+    for call_ in work:
+        call_()
     for tile in range(BAND):
-        at = tile * TILE
-        out[tile * 48 : tile * 48 + 32, :] = x_ref[at : at + TILE, :LANES]
-        out[tile * 48 + 32 : tile * 48 + 48, :] = x_ref[at : at + 16, LANES:] + pltpu.roll(
-            x_ref[at + 16 : at + 32, LANES:], 64, 1
+        at_ = tile * TILE
+        out[tile * 48 : tile * 48 + 32, :] = x_ref[at_ : at_ + TILE, :LANES]
+        out[tile * 48 + 32 : tile * 48 + 48, :] = x_ref[at_ : at_ + 16, LANES:] + pltpu.roll(
+            x_ref[at_ + 16 : at_ + 32, LANES:], 64, 1
         )
 
 
@@ -355,7 +397,9 @@
         [
             pltpu.VMEM((4, NB, LANES), f32),
             pltpu.VMEM((NB, 2 * LANES), f32),
-            pltpu.VMEM((LANES, LANES), f32),
+            pltpu.VMEM((4, LANES, LANES), f32),
+            pltpu.VMEM((4, 2, LANES, LANES), bf16),
+            pltpu.VMEM((4, 2, LANES, LANES), bf16),
             pltpu.VMEM((8, LANES), f32),
         ],
     )(core, mine, other, rows)

time: 169 us -> 165 us (0.976)
  Pallas kernels: 26.2 us -> 22.5 us
    pallas_call x1, Pallas kernels: 21.5 us -> 17.8 us  [do_solve(): call(solve_kernel, 'solve', (BAND * 48, LANES), [scalar(), whole(), whole...]
where the time goes in v4:
time: 165 us; the launch traced here: 163 us
  blocking collectives  132 us (80%)
  Pallas kernels  22.5 us (14%)
  starting transfers between devices  4.01 us (2%)
  waiting for transfers between devices  2.82 us (2%)
  local copies, waits for them, and re-layouts  1.73 us (1%)
    all_to_all x3, blocking collectives, exchange(): return lax.all_to_all(shaped, axis, 0, 0).reshape(rows.shape)  88.5 us
    pallas_call x1, Pallas kernels, do_solve(): call(solve_kernel, 'solve', (BAND * 48, LANES), [scalar(), whole(), whole...  17.8 us
    all_to_all x1, blocking collectives, gram_sum(): half = do_sum(lax.all_to_all(half, PLANE, 0, 0), depth, 1.0)  16.3 us
    all_to_all x1, blocking collectives, gram_sum(): return lax.all_to_all(half, PLANE, 0, 0).reshape(NB, LANES)  15.2 us
    all_to_all x1, blocking collectives, gram_sum(): half = do_sum(lax.all_to_all(half, 'z', 0, 0), IN_PLANE, 1.0 / NPTS)  11.5 us
    ppermute x2, starting transfers between devices, swap_cores(): return lax.ppermute(value, 'core', [(0, 1), (1, 0)])  4.01 us
  transfers between devices with their start and end apart: 2, of which 2 were waited for; matrix products, arithmetic and copies ran while one was open for 0% of the time, Pallas kernels for 0%

profile of v4, /device:TPU:6, one launch (start us, length us, event | category | flops | bytes accessed | tf_op | source)
XLA Modules:
  0.0 162.7 jit_solution(16974419323790549300)
XLA Ops:
  0.0 0.0 copy-start
  0.0 1.0 copy-done
  1.0 0.0 copy-start.3
  1.0 0.7 copy-done.3
  1.7 0.3 pack.1
  2.0 0.0 copy-start.1
  2.1 0.0 copy-start.2
  2.1 33.4 %all_to_all.30 = f32[32,48,128]{2,1,0:T(8,128)S(1)} all-to-all(f32[32,48,128]{2,1,0:T(8,128)S(1)} %bitcast.14), channel_id=1, replica_groups=mesh['y'=8,'xh'=2,'core'=2,'z'=8,'xl'=2] {'y','xh','core'}, dimensions={0} | all-to-all | bytes 1572864 | tf_op jit(solution)/shard_map/all_to_all | solution.py:414
  35.5 0.0 copy-done.1
  35.5 0.0 copy-done.2
  35.5 2.6 %filter.1 = f32[1024,128]{1,0:T(8,128)S(1)} custom-call(f32[1536,128]{1,0:T(8,128)S(1)} %bitcast.13, bf16[2,128,512]{2,1,0:T(8,128)(2,1)S(1)} %copy-done.1, bf16[2,192,192]{2,1,0:T(8,128)(2,1)S(1)} %copy-done.2), custom_call_target="tpu_custom_call" | custom-call | tf_op jit(solution)/shard_map/filter/pallas_call | solution.py:366
  38.1 37.4 %all_to_all.31 = f32[512,2,128]{2,1,0:T(2,128)S(1)} all-to-all(f32[512,2,128]{2,1,0:T(2,128)S(1)} %bitcast.15), channel_id=1, replica_groups=mesh['y'=8,'xh'=2,'core'=2,'z'=8,'xl'=2] {'z','xl','y','xh','core'}, dimensions={0} | all-to-all | bytes 1048576 | tf_op jit(solution)/shard_map/all_to_all | solution.py:414
  75.6 0.8 gram.1
  76.4 1.9 %collective-permute-start = (f32[512,128]{1,0:T(8,128)S(1)}, f32[512,128]{1,0:T(8,128)S(1)}, u32[]{:S(2)}, u32[]{:S(2)}) collective-permute-start(f32[512,128]{1,0:T(8,128)S(1)} %get-tuple-element.12), channel_id=1, source_target_pairs={{0,16},{16,0},{1,17},{17,1},{2,18},{18,2},{3,19},{19,3},{4,20},{20... | collective-permute-start | bytes 786440 | tf_op jit(solution)/shard_map/ppermute | solution.py:418
  78.3 1.5 collective-permute-done
  79.9 16.3 %all_to_all.32.parts = f32[32,16,128]{2,1,0:T(8,128)S(1)} all-to-all(f32[32,16,128]{2,1,0:T(8,128)S(1)} %bitcast.21), channel_id=1, replica_groups=mesh['y'=8,'xh'=2,'core'=2,'z'=8,'xl'=2] {'y','xh','xl'}, dimensions={0} | all-to-all | bytes 524288 | tf_op jit(solution)/shard_map/all_to_all | solution.py:424
  96.2 11.5 %all_to_all.33.parts = f32[8,16,128]{2,1,0:T(8,128)S(1)} all-to-all(f32[8,16,128]{2,1,0:T(8,128)S(1)} %sum.2), channel_id=1, replica_groups=mesh['y'=8,'xh'=2,'core'=2,'z'=8,'xl'=2] {'z'}, dimensions={0} | all-to-all | bytes 131072 | tf_op jit(solution)/shard_map/all_to_all | solution.py:425
  107.8 15.2 %all_to_all.34 = f32[32,16,128]{2,1,0:T(8,128)S(1)} all-to-all(f32[32,16,128]{2,1,0:T(8,128)S(1)} %sum.3), channel_id=1, replica_groups=mesh['y'=8,'xh'=2,'core'=2,'z'=8,'xl'=2] {'y','xh','xl'}, dimensions={0} | all-to-all | bytes 524288 | tf_op jit(solution)/shard_map/all_to_all | solution.py:426
  123.0 2.1 %collective-permute-start.1 = (f32[512,128]{1,0:T(8,128)S(1)}, f32[512,128]{1,0:T(8,128)S(1)}, u32[]{:S(2)}, u32[]{:S(2)}) collective-permute-start(f32[512,128]{1,0:T(8,128)S(1)} %bitcast.18), channel_id=1, source_target_pairs={{0,16},{16,0},{1,17},{17,1},{2,18},{18,2},{3,19},{19,3},{4,20},{20... | collective-permute-start | bytes 786440 | tf_op jit(solution)/shard_map/ppermute | solution.py:418
  125.1 1.3 collective-permute-done.1.other
  126.4 17.8 %solve.1 = f32[768,128]{1,0:T(8,128)S(1)} custom-call(s32[1]{0:T(128)} %bitcast.core, f32[512,128]{1,0:T(8,128)S(1)} %bitcast.19, f32[512,128]{1,0:T(8,128)S(1)} %collective-permute-done.1.other, f32[1024,128]{1,0:T(8,128)S(1)} %bitcast.12), custom_call_target="tpu_custom_call" | custom-call | tf_op jit(solution)/shard_map/solve/pallas_call | solution.py:392
  144.3 17.6 %all_to_all.35 = f32[16,48,128]{2,1,0:T(8,128)S(1)} all-to-all(f32[16,48,128]{2,1,0:T(8,128)S(1)} %bitcast.17), channel_id=1, replica_groups=mesh['y'=8,'xh'=2,'core'=2,'z'=8,'xl'=2] {'z','xl'}, dimensions={0} | all-to-all | bytes 786432 | tf_op jit(solution)/shard_map/all_to_all | solution.py:414
  161.9 0.8 unpack.1
  (3 shorter events, 0.1 us)
Async XLA Ops:
  0.0 1.0 copy-start
  1.0 0.7 copy-start.3
  2.0 33.5 %copy-start.1 = (bf16[2,128,512]{2,1,0:T(8,128)(2,1)S(1)}, bf16[2,128,512]{2,1,0:T(8,128)(2,1)}, u32[]{:S(2)}) copy-start(bf16[2,128,512]{2,1,0:T(8,128)(2,1)} %constant.10.clone.strip) | copy-start | bytes 786436
  2.1 33.5 %copy-start.2 = (bf16[2,192,192]{2,1,0:T(8,128)(2,1)S(1)}, bf16[2,192,192]{2,1,0:T(8,128)(2,1)}, u32[]{:S(2)}) copy-start(bf16[2,192,192]{2,1,0:T(8,128)(2,1)} %constant.11.clone.m_layer) | copy-start | bytes 442372
  76.4 3.4 %collective-permute-start = (f32[512,128]{1,0:T(8,128)S(1)}, f32[512,128]{1,0:T(8,128)S(1)}, u32[]{:S(2)}, u32[]{:S(2)}) collective-permute-start(f32[512,128]{1,0:T(8,128)S(1)} %get-tuple-element.12), channel_id=1, source_target_pairs={{0,16},{16,0},{1,17},{17,1},{2,18},{18,2},{3,19},{19,3},{4,20},{20... | collective-permute-start | bytes 786440 | tf_op jit(solution)/shard_map/ppermute | solution.py:418
  123.0 3.4 %collective-permute-start.1 = (f32[512,128]{1,0:T(8,128)S(1)}, f32[512,128]{1,0:T(8,128)S(1)}, u32[]{:S(2)}, u32[]{:S(2)}) collective-permute-start(f32[512,128]{1,0:T(8,128)S(1)} %bitcast.18), channel_id=1, source_target_pairs={{0,16},{16,0},{1,17},{17,1},{2,18},{18,2},{3,19},{19,3},{4,20},{20... | collective-permute-start | bytes 786440 | tf_op jit(solution)/shard_map/ppermute | solution.py:418

commit v5 on v4

--- a/solution.py
+++ b/solution.py
@@ -176,7 +176,7 @@
     return kernel
 
 
-def invert_block(m, ones, work):
+def invert_block(m, y_ref, ones, work):
     full = (8, LANES)
     sub = lax.broadcasted_iota(jnp.int32, full, 0)
     lane = lax.broadcasted_iota(jnp.int32, full, 1)
@@ -192,7 +192,23 @@
             (terms[4] + terms[5]) + (terms[6] + terms[7])
         )
 
+    def later(q, base, inside):
+        def update():
+            here = slice(8 * q, 8 * q + 8)
+            d = m[here, :]
+            terms = [
+                column(d, base + t) * y_ref[pl.ds(base + t, 8, stride=0), :] for t in range(8)
+            ]
+            m[here, :] = jnp.where(inside, 0.0, d) + total(terms)
+
+        return update
+
+    def some(calls, steps_left):
+        for _ in range(-(-len(calls) // steps_left)):
+            calls.pop(0)()
+
     v = m[0:8, :]
+    waiting = []
     for panel in range(16):
         base = 8 * panel
         inside = (lane >= base) & (lane < base + 8)
@@ -205,6 +221,12 @@
         for k in range(8):
             here = sub == k
             ahead = [row(a[k], j) for j in range(k)] + pivots[k:]
+            if k == 7:
+                masked = [jnp.where(here, 0.0, a[u]) for u in range(7)]
+                y = total([masked[u] * v_rows[u] for u in range(7)] + [jnp.zeros(full, f32)])
+                rest = v_rows[7] - total(
+                    [ahead[u] * v_rows[u] for u in range(7)] + [jnp.zeros(full, f32)]
+                )
             root = lax.rsqrt(ahead[k])
             inverse = root * root
             if k < 7:
@@ -215,28 +237,32 @@
                 lower[t] = jnp.where(here, a[t], lower[t])
             scale = jnp.where(here, root, scale)
             swept = jnp.where(here, -inverse, a[k] * inverse)
-            for j in range(8):
-                if j != k:
-                    a[j] = jnp.where(here, 0.0, a[j]) - swept * ahead[j]
-            a[k] = swept
-        y = total([a[u] * v_rows[u] for u in range(8)])
-        y_rows = [row(y, u) for u in range(8)]
+            if k < 7:
+                for j in range(8):
+                    if j != k:
+                        a[j] = jnp.where(here, 0.0, a[j]) - swept * ahead[j]
+                a[k] = swept
+                if k > 0:
+                    some(waiting, 7 - k)
+            else:
+                y = y + swept * rest
+        waiting = []
+        if panel < 15:
+            y_ref[base : base + 8, :] = y
+            d = m[base + 8 : base + 16, :]
+            terms = [column(d, base + t) * row(y, t) for t in range(8)]
+            following = jnp.where(inside, 0.0, d) + total(terms)
+            waiting = [later(q, base, inside) for q in range(panel + 2, 16)]
         done = v
         for t in range(7):
             done = done - lower[t] * v_rows[t]
         m[base : base + 8, :] = jnp.where(lane < base + 8, done * scale, 0.0)
-        for q in range(panel + 1, 16):
-            d = m[8 * q : 8 * q + 8, :]
-            d = jnp.where(inside, 0.0, d) + total([column(d, base + t) * y_rows[t] for t in range(8)])
-            if q == panel + 1:
-                v = d
-            else:
-                m[8 * q : 8 * q + 8, :] = d
-        for _ in range(-(-len(work) // (16 - panel))):
-            work.pop(0)()
-
-
-def solve_kernel(core, mine, other, rows, out, s_ref, x_ref, blocks, panels, inverses, ones_ref):
+        if panel < 15:
+            v = following
+        some(work, 16 - panel)
+
+
+def solve_kernel(core, mine, other, rows, out, s_ref, x_ref, blocks, panels, inverses, y_ref, ones_ref):
     first, second, raw = points_of(rows)
     x_ref[:, :LANES] = first
     x_ref[:, LANES:] = second
@@ -294,7 +320,7 @@
     work = []
     blocks[0] = s_ref[0, at(0), :]
     for j in range(4):
-        invert_block(blocks.at[j], ones, work)
+        invert_block(blocks.at[j], y_ref, ones, work)
         put(inverses, j, blocks[j])
         work = []
         if j < 3:
@@ -400,6 +426,7 @@
             pltpu.VMEM((4, LANES, LANES), f32),
             pltpu.VMEM((4, 2, LANES, LANES), bf16),
             pltpu.VMEM((4, 2, LANES, LANES), bf16),
+            pltpu.VMEM((LANES, LANES), f32),
             pltpu.VMEM((8, LANES), f32),
         ],
     )(core, mine, other, rows)

time: 165 us -> 162 us (0.982)
  Pallas kernels: 22.5 us -> 19.7 us
    pallas_call x1, Pallas kernels: 17.8 us -> 15.1 us  [do_solve(): call(solve_kernel, 'solve', (BAND * 48, LANES), [scalar(), whole(), whole...]
where the time goes in v5:
time: 162 us; the launch traced here: 160 us
  blocking collectives  132 us (81%)
  Pallas kernels  19.7 us (12%)
  starting transfers between devices  4.01 us (2%)
  waiting for transfers between devices  2.82 us (2%)
  local copies, waits for them, and re-layouts  1.73 us (1%)
    all_to_all x3, blocking collectives, exchange(): return lax.all_to_all(shaped, axis, 0, 0).reshape(rows.shape)  88.5 us
    all_to_all x1, blocking collectives, gram_sum(): half = do_sum(lax.all_to_all(half, PLANE, 0, 0), depth, 1.0)  16.3 us
    all_to_all x1, blocking collectives, gram_sum(): return lax.all_to_all(half, PLANE, 0, 0).reshape(NB, LANES)  15.2 us
    pallas_call x1, Pallas kernels, do_solve(): call(solve_kernel, 'solve', (BAND * 48, LANES), [scalar(), whole(), whole...  15.1 us
    all_to_all x1, blocking collectives, gram_sum(): half = do_sum(lax.all_to_all(half, 'z', 0, 0), IN_PLANE, 1.0 / NPTS)  11.5 us
    ppermute x2, starting transfers between devices, swap_cores(): return lax.ppermute(value, 'core', [(0, 1), (1, 0)])  4.01 us
  transfers between devices with their start and end apart: 2, of which 2 were waited for; matrix products, arithmetic and copies ran while one was open for 0% of the time, Pallas kernels for 0%

profile of v5, /device:TPU:6, one launch (start us, length us, event | category | flops | bytes accessed | tf_op | source)
XLA Modules:
  0.0 160.0 jit_solution(7034702656651811244)
XLA Ops:
  0.0 0.0 copy-start
  0.0 1.0 copy-done
  1.0 0.0 copy-start.3
  1.0 0.7 copy-done.3
  1.7 0.3 pack.1
  2.0 0.0 copy-start.1
  2.1 0.0 copy-start.2
  2.1 33.4 %all_to_all.30 = f32[32,48,128]{2,1,0:T(8,128)S(1)} all-to-all(f32[32,48,128]{2,1,0:T(8,128)S(1)} %bitcast.14), channel_id=1, replica_groups=mesh['y'=8,'xh'=2,'core'=2,'z'=8,'xl'=2] {'y','xh','core'}, dimensions={0} | all-to-all | bytes 1572864 | tf_op jit(solution)/shard_map/all_to_all | solution.py:441
  35.5 0.0 copy-done.1
  35.5 0.0 copy-done.2
  35.5 2.6 %filter.1 = f32[1024,128]{1,0:T(8,128)S(1)} custom-call(f32[1536,128]{1,0:T(8,128)S(1)} %bitcast.13, bf16[2,128,512]{2,1,0:T(8,128)(2,1)S(1)} %copy-done.1, bf16[2,192,192]{2,1,0:T(8,128)(2,1)S(1)} %copy-done.2), custom_call_target="tpu_custom_call" | custom-call | tf_op jit(solution)/shard_map/filter/pallas_call | solution.py:392
  38.1 37.4 %all_to_all.31 = f32[512,2,128]{2,1,0:T(2,128)S(1)} all-to-all(f32[512,2,128]{2,1,0:T(2,128)S(1)} %bitcast.15), channel_id=1, replica_groups=mesh['y'=8,'xh'=2,'core'=2,'z'=8,'xl'=2] {'z','xl','y','xh','core'}, dimensions={0} | all-to-all | bytes 1048576 | tf_op jit(solution)/shard_map/all_to_all | solution.py:441
  75.6 0.8 gram.1
  76.4 1.9 %collective-permute-start = (f32[512,128]{1,0:T(8,128)S(1)}, f32[512,128]{1,0:T(8,128)S(1)}, u32[]{:S(2)}, u32[]{:S(2)}) collective-permute-start(f32[512,128]{1,0:T(8,128)S(1)} %get-tuple-element.12), channel_id=1, source_target_pairs={{0,16},{16,0},{1,17},{17,1},{2,18},{18,2},{3,19},{19,3},{4,20},{20... | collective-permute-start | bytes 786440 | tf_op jit(solution)/shard_map/ppermute | solution.py:445
  78.3 1.5 collective-permute-done
  79.9 16.3 %all_to_all.32.parts = f32[32,16,128]{2,1,0:T(8,128)S(1)} all-to-all(f32[32,16,128]{2,1,0:T(8,128)S(1)} %bitcast.21), channel_id=1, replica_groups=mesh['y'=8,'xh'=2,'core'=2,'z'=8,'xl'=2] {'y','xh','xl'}, dimensions={0} | all-to-all | bytes 524288 | tf_op jit(solution)/shard_map/all_to_all | solution.py:451
  96.2 11.5 %all_to_all.33.parts = f32[8,16,128]{2,1,0:T(8,128)S(1)} all-to-all(f32[8,16,128]{2,1,0:T(8,128)S(1)} %sum.2), channel_id=1, replica_groups=mesh['y'=8,'xh'=2,'core'=2,'z'=8,'xl'=2] {'z'}, dimensions={0} | all-to-all | bytes 131072 | tf_op jit(solution)/shard_map/all_to_all | solution.py:452
  107.8 15.2 %all_to_all.34 = f32[32,16,128]{2,1,0:T(8,128)S(1)} all-to-all(f32[32,16,128]{2,1,0:T(8,128)S(1)} %sum.3), channel_id=1, replica_groups=mesh['y'=8,'xh'=2,'core'=2,'z'=8,'xl'=2] {'y','xh','xl'}, dimensions={0} | all-to-all | bytes 524288 | tf_op jit(solution)/shard_map/all_to_all | solution.py:453
  123.0 2.1 %collective-permute-start.1 = (f32[512,128]{1,0:T(8,128)S(1)}, f32[512,128]{1,0:T(8,128)S(1)}, u32[]{:S(2)}, u32[]{:S(2)}) collective-permute-start(f32[512,128]{1,0:T(8,128)S(1)} %bitcast.18), channel_id=1, source_target_pairs={{0,16},{16,0},{1,17},{17,1},{2,18},{18,2},{3,19},{19,3},{4,20},{20... | collective-permute-start | bytes 786440 | tf_op jit(solution)/shard_map/ppermute | solution.py:445
  125.1 1.3 collective-permute-done.1.other
  126.4 15.1 %solve.1 = f32[768,128]{1,0:T(8,128)S(1)} custom-call(s32[1]{0:T(128)} %bitcast.core, f32[512,128]{1,0:T(8,128)S(1)} %bitcast.19, f32[512,128]{1,0:T(8,128)S(1)} %collective-permute-done.1.other, f32[1024,128]{1,0:T(8,128)S(1)} %bitcast.12), custom_call_target="tpu_custom_call" | custom-call | tf_op jit(solution)/shard_map/solve/pallas_call | solution.py:418
  141.5 17.6 %all_to_all.35 = f32[16,48,128]{2,1,0:T(8,128)S(1)} all-to-all(f32[16,48,128]{2,1,0:T(8,128)S(1)} %bitcast.17), channel_id=1, replica_groups=mesh['y'=8,'xh'=2,'core'=2,'z'=8,'xl'=2] {'z','xl'}, dimensions={0} | all-to-all | bytes 786432 | tf_op jit(solution)/shard_map/all_to_all | solution.py:441
  159.1 0.8 unpack.1
  (3 shorter events, 0.1 us)
Async XLA Ops:
  0.0 1.0 copy-start
  1.0 0.7 copy-start.3
  2.0 33.5 %copy-start.1 = (bf16[2,128,512]{2,1,0:T(8,128)(2,1)S(1)}, bf16[2,128,512]{2,1,0:T(8,128)(2,1)}, u32[]{:S(2)}) copy-start(bf16[2,128,512]{2,1,0:T(8,128)(2,1)} %constant.10.clone.strip) | copy-start | bytes 786436
  2.1 33.5 %copy-start.2 = (bf16[2,192,192]{2,1,0:T(8,128)(2,1)S(1)}, bf16[2,192,192]{2,1,0:T(8,128)(2,1)}, u32[]{:S(2)}) copy-start(bf16[2,192,192]{2,1,0:T(8,128)(2,1)} %constant.11.clone.m_layer) | copy-start | bytes 442372
  76.4 3.4 %collective-permute-start = (f32[512,128]{1,0:T(8,128)S(1)}, f32[512,128]{1,0:T(8,128)S(1)}, u32[]{:S(2)}, u32[]{:S(2)}) collective-permute-start(f32[512,128]{1,0:T(8,128)S(1)} %get-tuple-element.12), channel_id=1, source_target_pairs={{0,16},{16,0},{1,17},{17,1},{2,18},{18,2},{3,19},{19,3},{4,20},{20... | collective-permute-start | bytes 786440 | tf_op jit(solution)/shard_map/ppermute | solution.py:445
  123.0 3.4 %collective-permute-start.1 = (f32[512,128]{1,0:T(8,128)S(1)}, f32[512,128]{1,0:T(8,128)S(1)}, u32[]{:S(2)}, u32[]{:S(2)}) collective-permute-start(f32[512,128]{1,0:T(8,128)S(1)} %bitcast.18), channel_id=1, source_target_pairs={{0,16},{16,0},{1,17},{17,1},{2,18},{18,2},{3,19},{19,3},{4,20},{20... | collective-permute-start | bytes 786440 | tf_op jit(solution)/shard_map/ppermute | solution.py:445

commit v6 on v5

--- a/solution.py
+++ b/solution.py
@@ -39,7 +39,6 @@
 CENTRE = 24.0
 HALF_WIDTH = 20.0
 
-HIGHEST = lax.Precision.HIGHEST
 f32 = jnp.float32
 bf16 = jnp.bfloat16
 
@@ -81,7 +80,17 @@
     return high, (value - high.astype(f32)).astype(bf16)
 
 
-def dot_split(left, right):
+NN = ((1,), (0,))
+NT = ((1,), (1,))
+
+
+def dot_split(left, right, dims):
+    a = jnp.concatenate([left[0], left[1], left[0]], axis=dims[0][0])
+    b = jnp.concatenate([right[1], right[0], right[0]], axis=dims[1][0])
+    return lax.dot_general(a, b, (dims, ((), ())), preferred_element_type=f32)
+
+
+def dot_apart(left, right):
     def dot(a, b):
         return jnp.dot(a, b, preferred_element_type=f32)
 
@@ -95,7 +104,7 @@
             row = layer * 8 + quarter
             out[pl.ds(row, TILE, stride=8 * DEPTH), :] = psi[layer, :, lanes]
             out[pl.ds(row + 4, TILE, stride=8 * DEPTH), :] = jnp.broadcast_to(
-                potential[layer : layer + 1, lanes] * (1.0 / HALF_WIDTH), (TILE, LANES)
+                potential[layer : layer + 1, lanes], (TILE, LANES)
             )
 
 
@@ -114,7 +123,7 @@
 
     def apply(values):
         pieces = split_value(values)
-        return dot_split(pieces, plane) + dot_split(layers, pieces) + potential * values
+        return dot_apart(pieces, plane) + dot_apart(layers, pieces) + potential * values
 
     previous = start
     current = apply(start)
@@ -146,20 +155,14 @@
     return first, jnp.where(lane < 64, second, 0.0), second
 
 
-def dot_nt(a, b):
-    return lax.dot_general(
-        a, b, (((1,), (1,)), ((), ())), precision=HIGHEST, preferred_element_type=f32
-    )
-
-
 def gram_kernel(core, rows, keep, send):
     first, second, _ = points_of(rows)
-    points = jnp.concatenate([first, second], axis=1)
-    low, high = points[:256], points[256:]
+    points = split_value(jnp.concatenate([first, second], axis=1))
+    low, high = [p[:256] for p in points], [p[256:] for p in points]
     row = lax.broadcasted_iota(jnp.int32, (256, 256), 0)
     col = lax.broadcasted_iota(jnp.int32, (256, 256), 1)
-    folded = jnp.where(col <= row, dot_nt(low, low), dot_nt(high, high))
-    below = dot_nt(high, low)
+    folded = jnp.where(col <= row, dot_split(low, low, NT), dot_split(high, high, NT))
+    below = dot_split(high, low, NT)
     first = core[0] == 0
     for half in range(2):
         lanes = slice(half * LANES, (half + 1) * LANES)
@@ -286,14 +289,6 @@
     def at(i):
         return slice(i * LANES, (i + 1) * LANES)
 
-    def split_dot(left, right, dims):
-        def dot(a, b):
-            return lax.dot_general(a, b, (dims, ((), ())), preferred_element_type=f32)
-
-        return (dot(left[0], right[1]) + dot(left[1], right[0])) + dot(left[0], right[0])
-
-    nt, nn = ((1,), (1,)), ((1,), (0,))
-
     def pieces(ref, i):
         return ref[i, 0], ref[i, 1]
 
@@ -301,19 +296,19 @@
         ref[i, 0], ref[i, 1] = split_value(value)
 
     def form_panel(j, i):
-        put(panels, i, split_dot(split_value(s_ref[j, at(i), :]), pieces(inverses, j), nt))
+        put(panels, i, dot_split(split_value(s_ref[j, at(i), :]), pieces(inverses, j), NT))
 
     def update_s(k, i):
-        s_ref[k, at(i), :] = s_ref[k, at(i), :] - split_dot(
-            pieces(panels, i), pieces(panels, k), nt
+        s_ref[k, at(i), :] = s_ref[k, at(i), :] - dot_split(
+            pieces(panels, i), pieces(panels, k), NT
         )
 
     def solve_x(j):
-        x_ref[at(j), :] = split_dot(pieces(inverses, j), split_value(x_ref[at(j), :]), nn)
+        x_ref[at(j), :] = dot_split(pieces(inverses, j), split_value(x_ref[at(j), :]), NN)
 
     def update_x(j, i):
-        x_ref[at(i), :] = x_ref[at(i), :] - split_dot(
-            pieces(panels, i), split_value(x_ref[at(j), :]), nn
+        x_ref[at(i), :] = x_ref[at(i), :] - dot_split(
+            pieces(panels, i), split_value(x_ref[at(j), :]), NN
         )
 
     ones = ones_ref[...]
@@ -325,8 +320,8 @@
         work = []
         if j < 3:
             form_panel(j, j + 1)
-            blocks[j + 1] = s_ref[j + 1, at(j + 1), :] - split_dot(
-                pieces(panels, j + 1), pieces(panels, j + 1), nt
+            blocks[j + 1] = s_ref[j + 1, at(j + 1), :] - dot_split(
+                pieces(panels, j + 1), pieces(panels, j + 1), NT
             )
             for i in range(j + 2, 4):
                 work.append(lambda j=j, i=i: form_panel(j, i))
@@ -456,7 +451,7 @@
 def shards(psi, potential):
     core = lax.axis_index("core").astype(jnp.int32).reshape(1)
     psi, core = lax.optimization_barrier((psi, core))
-    bands = exchange(do_pack(jnp.transpose(psi, (1, 0, 2)), potential), LAYERS, DOM)
+    bands = exchange(do_pack(jnp.transpose(psi, (1, 0, 2)), potential * (1.0 / HALF_WIDTH)), LAYERS, DOM)
     points = exchange(do_filter(bands), ALL, NB)
     gram = gram_sum(*do_gram(core, points))
     result = exchange(do_solve(core, gram, swap_cores(gram), points), BANDS, BAND)

time: 162 us -> 161 us (level)
  no operation moved by 1% of the time
where the time goes in v6:
time: 161 us; the launch traced here: 159 us
  blocking collectives  132 us (82%)
  Pallas kernels  18.7 us (12%)
  starting transfers between devices  4.01 us (2%)
  waiting for transfers between devices  2.82 us (2%)
    all_to_all x3, blocking collectives, exchange(): return lax.all_to_all(shaped, axis, 0, 0).reshape(rows.shape)  88.5 us
    all_to_all x1, blocking collectives, gram_sum(): half = do_sum(lax.all_to_all(half, PLANE, 0, 0), depth, 1.0)  16.3 us
    all_to_all x1, blocking collectives, gram_sum(): return lax.all_to_all(half, PLANE, 0, 0).reshape(NB, LANES)  15.2 us
    pallas_call x1, Pallas kernels, do_solve(): call(solve_kernel, 'solve', (BAND * 48, LANES), [scalar(), whole(), whole...  14.3 us
    all_to_all x1, blocking collectives, gram_sum(): half = do_sum(lax.all_to_all(half, 'z', 0, 0), IN_PLANE, 1.0 / NPTS)  11.5 us
    ppermute x2, starting transfers between devices, swap_cores(): return lax.ppermute(value, 'core', [(0, 1), (1, 0)])  4.01 us
  transfers between devices with their start and end apart: 2, of which 2 were waited for; matrix products, arithmetic and copies ran while one was open for 0% of the time, Pallas kernels for 0%

profile of v6, /device:TPU:6, one launch (start us, length us, event | category | flops | bytes accessed | tf_op | source)
XLA Modules:
  0.0 158.9 jit_solution(8071646533977782526)
XLA Ops:
  0.0 0.7 broadcast_multiply_fusion.potential
  0.7 0.0 copy-start
  0.7 1.0 copy-done
  1.7 0.3 pack.1
  2.0 0.0 copy-start.1
  2.0 0.0 copy-start.2
  2.1 33.4 %all_to_all.30 = f32[32,48,128]{2,1,0:T(8,128)S(1)} all-to-all(f32[32,48,128]{2,1,0:T(8,128)S(1)} %bitcast.14), channel_id=1, replica_groups=mesh['y'=8,'xh'=2,'core'=2,'z'=8,'xl'=2] {'y','xh','core'}, dimensions={0} | all-to-all | bytes 1572864 | tf_op jit(solution)/shard_map/all_to_all | solution.py:436
  35.5 0.0 copy-done.1
  35.5 0.0 copy-done.2
  35.5 2.6 %filter.1 = f32[1024,128]{1,0:T(8,128)S(1)} custom-call(f32[1536,128]{1,0:T(8,128)S(1)} %bitcast.13, bf16[2,128,512]{2,1,0:T(8,128)(2,1)S(1)} %copy-done.1, bf16[2,192,192]{2,1,0:T(8,128)(2,1)S(1)} %copy-done.2), custom_call_target="tpu_custom_call" | custom-call | tf_op jit(solution)/shard_map/filter/pallas_call | solution.py:387
  38.1 37.4 %all_to_all.31 = f32[512,2,128]{2,1,0:T(2,128)S(1)} all-to-all(f32[512,2,128]{2,1,0:T(2,128)S(1)} %bitcast.15), channel_id=1, replica_groups=mesh['y'=8,'xh'=2,'core'=2,'z'=8,'xl'=2] {'z','xl','y','xh','core'}, dimensions={0} | all-to-all | bytes 1048576 | tf_op jit(solution)/shard_map/all_to_all | solution.py:436
  75.6 0.5 gram.1
  76.1 1.9 %collective-permute-start = (f32[512,128]{1,0:T(8,128)S(1)}, f32[512,128]{1,0:T(8,128)S(1)}, u32[]{:S(2)}, u32[]{:S(2)}) collective-permute-start(f32[512,128]{1,0:T(8,128)S(1)} %get-tuple-element.12), channel_id=1, source_target_pairs={{0,16},{16,0},{1,17},{17,1},{2,18},{18,2},{3,19},{19,3},{4,20},{20... | collective-permute-start | bytes 786440 | tf_op jit(solution)/shard_map/ppermute | solution.py:440
  78.0 1.5 collective-permute-done
  79.6 16.3 %all_to_all.32.parts = f32[32,16,128]{2,1,0:T(8,128)S(1)} all-to-all(f32[32,16,128]{2,1,0:T(8,128)S(1)} %bitcast.21), channel_id=1, replica_groups=mesh['y'=8,'xh'=2,'core'=2,'z'=8,'xl'=2] {'y','xh','xl'}, dimensions={0} | all-to-all | bytes 524288 | tf_op jit(solution)/shard_map/all_to_all | solution.py:446
  95.9 11.5 %all_to_all.33.parts = f32[8,16,128]{2,1,0:T(8,128)S(1)} all-to-all(f32[8,16,128]{2,1,0:T(8,128)S(1)} %sum.2), channel_id=1, replica_groups=mesh['y'=8,'xh'=2,'core'=2,'z'=8,'xl'=2] {'z'}, dimensions={0} | all-to-all | bytes 131072 | tf_op jit(solution)/shard_map/all_to_all | solution.py:447
  107.5 15.2 %all_to_all.34 = f32[32,16,128]{2,1,0:T(8,128)S(1)} all-to-all(f32[32,16,128]{2,1,0:T(8,128)S(1)} %sum.3), channel_id=1, replica_groups=mesh['y'=8,'xh'=2,'core'=2,'z'=8,'xl'=2] {'y','xh','xl'}, dimensions={0} | all-to-all | bytes 524288 | tf_op jit(solution)/shard_map/all_to_all | solution.py:448
  122.7 2.1 %collective-permute-start.1 = (f32[512,128]{1,0:T(8,128)S(1)}, f32[512,128]{1,0:T(8,128)S(1)}, u32[]{:S(2)}, u32[]{:S(2)}) collective-permute-start(f32[512,128]{1,0:T(8,128)S(1)} %bitcast.18), channel_id=1, source_target_pairs={{0,16},{16,0},{1,17},{17,1},{2,18},{18,2},{3,19},{19,3},{4,20},{20... | collective-permute-start | bytes 786440 | tf_op jit(solution)/shard_map/ppermute | solution.py:440
  124.8 1.3 collective-permute-done.1.other
  126.1 14.3 %solve.1 = f32[768,128]{1,0:T(8,128)S(1)} custom-call(s32[1]{0:T(128)} %bitcast.core, f32[512,128]{1,0:T(8,128)S(1)} %bitcast.19, f32[512,128]{1,0:T(8,128)S(1)} %collective-permute-done.1.other, f32[1024,128]{1,0:T(8,128)S(1)} %bitcast.12), custom_call_target="tpu_custom_call" | custom-call | tf_op jit(solution)/shard_map/solve/pallas_call | solution.py:413
  140.5 17.6 %all_to_all.35 = f32[16,48,128]{2,1,0:T(8,128)S(1)} all-to-all(f32[16,48,128]{2,1,0:T(8,128)S(1)} %bitcast.17), channel_id=1, replica_groups=mesh['y'=8,'xh'=2,'core'=2,'z'=8,'xl'=2] {'z','xl'}, dimensions={0} | all-to-all | bytes 786432 | tf_op jit(solution)/shard_map/all_to_all | solution.py:436
  158.1 0.8 unpack.1
  (3 shorter events, 0.1 us)
Async XLA Ops:
  0.7 1.0 copy-start
  2.0 33.5 %copy-start.1 = (bf16[2,128,512]{2,1,0:T(8,128)(2,1)S(1)}, bf16[2,128,512]{2,1,0:T(8,128)(2,1)}, u32[]{:S(2)}) copy-start(bf16[2,128,512]{2,1,0:T(8,128)(2,1)} %constant.12.clone.strip) | copy-start | bytes 786436
  2.0 33.5 %copy-start.2 = (bf16[2,192,192]{2,1,0:T(8,128)(2,1)S(1)}, bf16[2,192,192]{2,1,0:T(8,128)(2,1)}, u32[]{:S(2)}) copy-start(bf16[2,192,192]{2,1,0:T(8,128)(2,1)} %constant.13.clone.m_layer) | copy-start | bytes 442372
  76.1 3.4 %collective-permute-start = (f32[512,128]{1,0:T(8,128)S(1)}, f32[512,128]{1,0:T(8,128)S(1)}, u32[]{:S(2)}, u32[]{:S(2)}) collective-permute-start(f32[512,128]{1,0:T(8,128)S(1)} %get-tuple-element.12), channel_id=1, source_target_pairs={{0,16},{16,0},{1,17},{17,1},{2,18},{18,2},{3,19},{19,3},{4,20},{20... | collective-permute-start | bytes 786440 | tf_op jit(solution)/shard_map/ppermute | solution.py:440
  122.7 3.4 %collective-permute-start.1 = (f32[512,128]{1,0:T(8,128)S(1)}, f32[512,128]{1,0:T(8,128)S(1)}, u32[]{:S(2)}, u32[]{:S(2)}) collective-permute-start(f32[512,128]{1,0:T(8,128)S(1)} %bitcast.18), channel_id=1, source_target_pairs={{0,16},{16,0},{1,17},{17,1},{2,18},{18,2},{3,19},{19,3},{4,20},{20... | collective-permute-start | bytes 786440 | tf_op jit(solution)/shard_map/ppermute | solution.py:440

commit v7 on v6

--- a/solution.py
+++ b/solution.py
@@ -23,7 +23,8 @@
 LAYERS = ("y", "xh", "core")
 BANDS = ("z", "xl")
 ALL = BANDS + LAYERS
-PLANE = ("y", "xh", "xl")
+PLANE = ("xl", "y", "xh")
+BACK = ("xl", "z")
 IN_PLANE = 32
 
 COEF = (
@@ -336,23 +337,30 @@
         call_()
     for tile in range(BAND):
         at_ = tile * TILE
-        out[tile * 48 : tile * 48 + 32, :] = x_ref[at_ : at_ + TILE, :LANES]
-        out[tile * 48 + 32 : tile * 48 + 48, :] = x_ref[at_ : at_ + 16, LANES:] + pltpu.roll(
+        to = place(tile) * 48
+        out[to : to + 32, :] = x_ref[at_ : at_ + TILE, :LANES]
+        out[to + 32 : to + 48, :] = x_ref[at_ : at_ + 16, LANES:] + pltpu.roll(
             x_ref[at_ + 16 : at_ + 32, LANES:], 64, 1
         )
+
+
+def place(tile):
+    return (tile % 2) * (BAND // 2) + tile // 2
 
 
 def unpack_kernel(rows, out):
     for piece in range(BAND):
         quarter = piece % 4
         out[piece // 4, :, quarter * LANES : (quarter + 1) * LANES] = rows[
-            piece * 48 : piece * 48 + 32, :
+            place(piece) * 48 : place(piece) * 48 + 32, :
         ]
     lower = lax.broadcasted_iota(jnp.int32, (16, LANES), 1) < 64
     for half in range(8):
         lanes = slice((half % 4) * LANES, (half % 4 + 1) * LANES)
-        even = rows[2 * half * 48 + 32 : 2 * half * 48 + 48, :]
-        odd = rows[(2 * half + 1) * 48 + 32 : (2 * half + 1) * 48 + 48, :]
+        even, odd = (
+            rows[place(piece) * 48 + 32 : place(piece) * 48 + 48, :]
+            for piece in (2 * half, 2 * half + 1)
+        )
         out[4 + half // 4, 0:16, lanes] = jnp.where(lower, even, pltpu.roll(odd, 64, 1))
         out[4 + half // 4, 16:32, lanes] = jnp.where(lower, pltpu.roll(even, 64, 1), odd)
 
@@ -454,7 +462,7 @@
     bands = exchange(do_pack(jnp.transpose(psi, (1, 0, 2)), potential * (1.0 / HALF_WIDTH)), LAYERS, DOM)
     points = exchange(do_filter(bands), ALL, NB)
     gram = gram_sum(*do_gram(core, points))
-    result = exchange(do_solve(core, gram, swap_cores(gram), points), BANDS, BAND)
+    result = exchange(do_solve(core, gram, swap_cores(gram), points), BACK, BAND)
     return jnp.transpose(do_unpack(result), (1, 0, 2))
 
 

time: 161 us -> 159 us (0.988)
  blocking collectives: 132 us -> 130 us
where the time goes in v7:
time: 159 us; the launch traced here: 157 us
  blocking collectives  130 us (82%)
  Pallas kernels  18.7 us (12%)
  starting transfers between devices  4.01 us (3%)
  waiting for transfers between devices  2.82 us (2%)
    all_to_all x3, blocking collectives, exchange(): return lax.all_to_all(shaped, axis, 0, 0).reshape(rows.shape)  87.4 us
    all_to_all x1, blocking collectives, gram_sum(): half = do_sum(lax.all_to_all(half, PLANE, 0, 0), depth, 1.0)  16.1 us
    all_to_all x1, blocking collectives, gram_sum(): return lax.all_to_all(half, PLANE, 0, 0).reshape(NB, LANES)  15.2 us
    pallas_call x1, Pallas kernels, do_solve(): call(solve_kernel, 'solve', (BAND * 48, LANES), [scalar(), whole(), whole...  14.3 us
    all_to_all x1, blocking collectives, gram_sum(): half = do_sum(lax.all_to_all(half, 'z', 0, 0), IN_PLANE, 1.0 / NPTS)  11.4 us
    ppermute x2, starting transfers between devices, swap_cores(): return lax.ppermute(value, 'core', [(0, 1), (1, 0)])  4.01 us
  transfers between devices with their start and end apart: 2, of which 2 were waited for; matrix products, arithmetic and copies ran while one was open for 0% of the time, Pallas kernels for 0%

profile of v7, /device:TPU:6, one launch (start us, length us, event | category | flops | bytes accessed | tf_op | source)
XLA Modules:
  0.0 157.4 jit_solution(13403936765889334219)
XLA Ops:
  0.0 0.7 broadcast_multiply_fusion.potential
  0.7 0.0 copy-start
  0.7 1.0 copy-done
  1.7 0.3 pack.1
  2.0 0.0 copy-start.1
  2.0 0.0 copy-start.2
  2.1 33.4 %all_to_all.30 = f32[32,48,128]{2,1,0:T(8,128)S(1)} all-to-all(f32[32,48,128]{2,1,0:T(8,128)S(1)} %bitcast.14), channel_id=1, replica_groups=mesh['y'=8,'xh'=2,'core'=2,'z'=8,'xl'=2] {'y','xh','core'}, dimensions={0} | all-to-all | bytes 1572864 | tf_op jit(solution)/shard_map/all_to_all | solution.py:444
  35.5 0.0 copy-done.1
  35.5 0.0 copy-done.2
  35.5 2.6 %filter.1 = f32[1024,128]{1,0:T(8,128)S(1)} custom-call(f32[1536,128]{1,0:T(8,128)S(1)} %bitcast.13, bf16[2,128,512]{2,1,0:T(8,128)(2,1)S(1)} %copy-done.1, bf16[2,192,192]{2,1,0:T(8,128)(2,1)S(1)} %copy-done.2), custom_call_target="tpu_custom_call" | custom-call | tf_op jit(solution)/shard_map/filter/pallas_call | solution.py:395
  38.1 37.4 %all_to_all.31 = f32[512,2,128]{2,1,0:T(2,128)S(1)} all-to-all(f32[512,2,128]{2,1,0:T(2,128)S(1)} %bitcast.15), channel_id=1, replica_groups=mesh['y'=8,'xh'=2,'core'=2,'z'=8,'xl'=2] {'z','xl','y','xh','core'}, dimensions={0} | all-to-all | bytes 1048576 | tf_op jit(solution)/shard_map/all_to_all | solution.py:444
  75.6 0.5 gram.1
  76.1 1.9 %collective-permute-start = (f32[512,128]{1,0:T(8,128)S(1)}, f32[512,128]{1,0:T(8,128)S(1)}, u32[]{:S(2)}, u32[]{:S(2)}) collective-permute-start(f32[512,128]{1,0:T(8,128)S(1)} %get-tuple-element.12), channel_id=1, source_target_pairs={{0,16},{16,0},{1,17},{17,1},{2,18},{18,2},{3,19},{19,3},{4,20},{20... | collective-permute-start | bytes 786440 | tf_op jit(solution)/shard_map/ppermute | solution.py:448
  78.0 1.5 collective-permute-done
  79.6 16.1 %all_to_all.32.parts = f32[32,16,128]{2,1,0:T(8,128)S(1)} all-to-all(f32[32,16,128]{2,1,0:T(8,128)S(1)} %bitcast.21), channel_id=1, replica_groups=mesh['y'=8,'xh'=2,'core'=2,'z'=8,'xl'=2] {'xl','y','xh'}, dimensions={0} | all-to-all | bytes 524288 | tf_op jit(solution)/shard_map/all_to_all | solution.py:454
  95.7 11.4 %all_to_all.33.parts = f32[8,16,128]{2,1,0:T(8,128)S(1)} all-to-all(f32[8,16,128]{2,1,0:T(8,128)S(1)} %sum.2), channel_id=1, replica_groups=mesh['y'=8,'xh'=2,'core'=2,'z'=8,'xl'=2] {'z'}, dimensions={0} | all-to-all | bytes 131072 | tf_op jit(solution)/shard_map/all_to_all | solution.py:455
  107.1 15.2 %all_to_all.34 = f32[32,16,128]{2,1,0:T(8,128)S(1)} all-to-all(f32[32,16,128]{2,1,0:T(8,128)S(1)} %sum.3), channel_id=1, replica_groups=mesh['y'=8,'xh'=2,'core'=2,'z'=8,'xl'=2] {'xl','y','xh'}, dimensions={0} | all-to-all | bytes 524288 | tf_op jit(solution)/shard_map/all_to_all | solution.py:456
  122.3 2.1 %collective-permute-start.1 = (f32[512,128]{1,0:T(8,128)S(1)}, f32[512,128]{1,0:T(8,128)S(1)}, u32[]{:S(2)}, u32[]{:S(2)}) collective-permute-start(f32[512,128]{1,0:T(8,128)S(1)} %bitcast.18), channel_id=1, source_target_pairs={{0,16},{16,0},{1,17},{17,1},{2,18},{18,2},{3,19},{19,3},{4,20},{20... | collective-permute-start | bytes 786440 | tf_op jit(solution)/shard_map/ppermute | solution.py:448
  124.4 1.3 collective-permute-done.1.other
  125.7 14.3 %solve.1 = f32[768,128]{1,0:T(8,128)S(1)} custom-call(s32[1]{0:T(128)} %bitcast.core, f32[512,128]{1,0:T(8,128)S(1)} %bitcast.19, f32[512,128]{1,0:T(8,128)S(1)} %collective-permute-done.1.other, f32[1024,128]{1,0:T(8,128)S(1)} %bitcast.12), custom_call_target="tpu_custom_call" | custom-call | tf_op jit(solution)/shard_map/solve/pallas_call | solution.py:421
  140.0 16.5 %all_to_all.35 = f32[16,48,128]{2,1,0:T(8,128)S(1)} all-to-all(f32[16,48,128]{2,1,0:T(8,128)S(1)} %bitcast.17), channel_id=1, replica_groups=mesh['y'=8,'xh'=2,'core'=2,'z'=8,'xl'=2] {'xl','z'}, dimensions={0} | all-to-all | bytes 786432 | tf_op jit(solution)/shard_map/all_to_all | solution.py:444
  156.6 0.8 unpack.1
  (3 shorter events, 0.1 us)
Async XLA Ops:
  0.7 1.0 copy-start
  2.0 33.5 %copy-start.1 = (bf16[2,128,512]{2,1,0:T(8,128)(2,1)S(1)}, bf16[2,128,512]{2,1,0:T(8,128)(2,1)}, u32[]{:S(2)}) copy-start(bf16[2,128,512]{2,1,0:T(8,128)(2,1)} %constant.12.clone.strip) | copy-start | bytes 786436
  2.0 33.5 %copy-start.2 = (bf16[2,192,192]{2,1,0:T(8,128)(2,1)S(1)}, bf16[2,192,192]{2,1,0:T(8,128)(2,1)}, u32[]{:S(2)}) copy-start(bf16[2,192,192]{2,1,0:T(8,128)(2,1)} %constant.13.clone.m_layer) | copy-start | bytes 442372
  76.1 3.4 %collective-permute-start = (f32[512,128]{1,0:T(8,128)S(1)}, f32[512,128]{1,0:T(8,128)S(1)}, u32[]{:S(2)}, u32[]{:S(2)}) collective-permute-start(f32[512,128]{1,0:T(8,128)S(1)} %get-tuple-element.12), channel_id=1, source_target_pairs={{0,16},{16,0},{1,17},{17,1},{2,18},{18,2},{3,19},{19,3},{4,20},{20... | collective-permute-start | bytes 786440 | tf_op jit(solution)/shard_map/ppermute | solution.py:448
  122.3 3.4 %collective-permute-start.1 = (f32[512,128]{1,0:T(8,128)S(1)}, f32[512,128]{1,0:T(8,128)S(1)}, u32[]{:S(2)}, u32[]{:S(2)}) collective-permute-start(f32[512,128]{1,0:T(8,128)S(1)} %bitcast.18), channel_id=1, source_target_pairs={{0,16},{16,0},{1,17},{17,1},{2,18},{18,2},{3,19},{19,3},{4,20},{20... | collective-permute-start | bytes 786440 | tf_op jit(solution)/shard_map/ppermute | solution.py:448

commit v8 on v7

--- a/solution.py
+++ b/solution.py
@@ -23,7 +23,7 @@
 LAYERS = ("y", "xh", "core")
 BANDS = ("z", "xl")
 ALL = BANDS + LAYERS
-PLANE = ("xl", "y", "xh")
+PLANE = ("y", "xh", "xl")
 BACK = ("xl", "z")
 IN_PLANE = 32
 

time: 159 us -> 159 us (level)
  no operation moved by 1% of the time
where the time goes in v8:
time: 159 us; the launch traced here: 157 us
  blocking collectives  130 us (82%)
  Pallas kernels  18.7 us (12%)
  starting transfers between devices  4.01 us (3%)
  waiting for transfers between devices  2.82 us (2%)
    all_to_all x3, blocking collectives, exchange(): return lax.all_to_all(shaped, axis, 0, 0).reshape(rows.shape)  86.7 us
    all_to_all x1, blocking collectives, gram_sum(): half = do_sum(lax.all_to_all(half, PLANE, 0, 0), depth, 1.0)  16.3 us
    all_to_all x1, blocking collectives, gram_sum(): return lax.all_to_all(half, PLANE, 0, 0).reshape(NB, LANES)  15.2 us
    pallas_call x1, Pallas kernels, do_solve(): call(solve_kernel, 'solve', (BAND * 48, LANES), [scalar(), whole(), whole...  14.3 us
    all_to_all x1, blocking collectives, gram_sum(): half = do_sum(lax.all_to_all(half, 'z', 0, 0), IN_PLANE, 1.0 / NPTS)  11.5 us
    ppermute x2, starting transfers between devices, swap_cores(): return lax.ppermute(value, 'core', [(0, 1), (1, 0)])  4.01 us
  transfers between devices with their start and end apart: 2, of which 2 were waited for; matrix products, arithmetic and copies ran while one was open for 0% of the time, Pallas kernels for 0%

profile of v8, /device:TPU:6, one launch (start us, length us, event | category | flops | bytes accessed | tf_op | source)
XLA Modules:
  0.0 157.1 jit_solution(8792988299821114345)
XLA Ops:
  0.0 0.7 broadcast_multiply_fusion.potential
  0.7 0.0 copy-start
  0.7 1.0 copy-done
  1.7 0.3 pack.1
  2.0 0.0 copy-start.1
  2.0 0.0 copy-start.2
  2.1 33.4 %all_to_all.30 = f32[32,48,128]{2,1,0:T(8,128)S(1)} all-to-all(f32[32,48,128]{2,1,0:T(8,128)S(1)} %bitcast.14), channel_id=1, replica_groups=mesh['y'=8,'xh'=2,'core'=2,'z'=8,'xl'=2] {'y','xh','core'}, dimensions={0} | all-to-all | bytes 1572864 | tf_op jit(solution)/shard_map/all_to_all | solution.py:444
  35.5 0.0 copy-done.1
  35.5 0.0 copy-done.2
  35.5 2.6 %filter.1 = f32[1024,128]{1,0:T(8,128)S(1)} custom-call(f32[1536,128]{1,0:T(8,128)S(1)} %bitcast.13, bf16[2,128,512]{2,1,0:T(8,128)(2,1)S(1)} %copy-done.1, bf16[2,192,192]{2,1,0:T(8,128)(2,1)S(1)} %copy-done.2), custom_call_target="tpu_custom_call" | custom-call | tf_op jit(solution)/shard_map/filter/pallas_call | solution.py:395
  38.1 37.4 %all_to_all.31 = f32[512,2,128]{2,1,0:T(2,128)S(1)} all-to-all(f32[512,2,128]{2,1,0:T(2,128)S(1)} %bitcast.15), channel_id=1, replica_groups=mesh['y'=8,'xh'=2,'core'=2,'z'=8,'xl'=2] {'z','xl','y','xh','core'}, dimensions={0} | all-to-all | bytes 1048576 | tf_op jit(solution)/shard_map/all_to_all | solution.py:444
  75.6 0.5 gram.1
  76.1 1.9 %collective-permute-start = (f32[512,128]{1,0:T(8,128)S(1)}, f32[512,128]{1,0:T(8,128)S(1)}, u32[]{:S(2)}, u32[]{:S(2)}) collective-permute-start(f32[512,128]{1,0:T(8,128)S(1)} %get-tuple-element.12), channel_id=1, source_target_pairs={{0,16},{16,0},{1,17},{17,1},{2,18},{18,2},{3,19},{19,3},{4,20},{20... | collective-permute-start | bytes 786440 | tf_op jit(solution)/shard_map/ppermute | solution.py:448
  78.0 1.5 collective-permute-done
  79.6 16.3 %all_to_all.32.parts = f32[32,16,128]{2,1,0:T(8,128)S(1)} all-to-all(f32[32,16,128]{2,1,0:T(8,128)S(1)} %bitcast.21), channel_id=1, replica_groups=mesh['y'=8,'xh'=2,'core'=2,'z'=8,'xl'=2] {'y','xh','xl'}, dimensions={0} | all-to-all | bytes 524288 | tf_op jit(solution)/shard_map/all_to_all | solution.py:454
  95.9 11.5 %all_to_all.33.parts = f32[8,16,128]{2,1,0:T(8,128)S(1)} all-to-all(f32[8,16,128]{2,1,0:T(8,128)S(1)} %sum.2), channel_id=1, replica_groups=mesh['y'=8,'xh'=2,'core'=2,'z'=8,'xl'=2] {'z'}, dimensions={0} | all-to-all | bytes 131072 | tf_op jit(solution)/shard_map/all_to_all | solution.py:455
  107.5 15.2 %all_to_all.34 = f32[32,16,128]{2,1,0:T(8,128)S(1)} all-to-all(f32[32,16,128]{2,1,0:T(8,128)S(1)} %sum.3), channel_id=1, replica_groups=mesh['y'=8,'xh'=2,'core'=2,'z'=8,'xl'=2] {'y','xh','xl'}, dimensions={0} | all-to-all | bytes 524288 | tf_op jit(solution)/shard_map/all_to_all | solution.py:456
  122.7 2.1 %collective-permute-start.1 = (f32[512,128]{1,0:T(8,128)S(1)}, f32[512,128]{1,0:T(8,128)S(1)}, u32[]{:S(2)}, u32[]{:S(2)}) collective-permute-start(f32[512,128]{1,0:T(8,128)S(1)} %bitcast.18), channel_id=1, source_target_pairs={{0,16},{16,0},{1,17},{17,1},{2,18},{18,2},{3,19},{19,3},{4,20},{20... | collective-permute-start | bytes 786440 | tf_op jit(solution)/shard_map/ppermute | solution.py:448
  124.8 1.3 collective-permute-done.1.other
  126.1 14.3 %solve.1 = f32[768,128]{1,0:T(8,128)S(1)} custom-call(s32[1]{0:T(128)} %bitcast.core, f32[512,128]{1,0:T(8,128)S(1)} %bitcast.19, f32[512,128]{1,0:T(8,128)S(1)} %collective-permute-done.1.other, f32[1024,128]{1,0:T(8,128)S(1)} %bitcast.12), custom_call_target="tpu_custom_call" | custom-call | tf_op jit(solution)/shard_map/solve/pallas_call | solution.py:421
  140.5 15.8 %all_to_all.35 = f32[16,48,128]{2,1,0:T(8,128)S(1)} all-to-all(f32[16,48,128]{2,1,0:T(8,128)S(1)} %bitcast.17), channel_id=1, replica_groups=mesh['y'=8,'xh'=2,'core'=2,'z'=8,'xl'=2] {'xl','z'}, dimensions={0} | all-to-all | bytes 786432 | tf_op jit(solution)/shard_map/all_to_all | solution.py:444
  156.3 0.8 unpack.1
  (3 shorter events, 0.1 us)
Async XLA Ops:
  0.7 1.0 copy-start
  2.0 33.5 %copy-start.1 = (bf16[2,128,512]{2,1,0:T(8,128)(2,1)S(1)}, bf16[2,128,512]{2,1,0:T(8,128)(2,1)}, u32[]{:S(2)}) copy-start(bf16[2,128,512]{2,1,0:T(8,128)(2,1)} %constant.12.clone.strip) | copy-start | bytes 786436
  2.0 33.5 %copy-start.2 = (bf16[2,192,192]{2,1,0:T(8,128)(2,1)S(1)}, bf16[2,192,192]{2,1,0:T(8,128)(2,1)}, u32[]{:S(2)}) copy-start(bf16[2,192,192]{2,1,0:T(8,128)(2,1)} %constant.13.clone.m_layer) | copy-start | bytes 442372
  76.1 3.4 %collective-permute-start = (f32[512,128]{1,0:T(8,128)S(1)}, f32[512,128]{1,0:T(8,128)S(1)}, u32[]{:S(2)}, u32[]{:S(2)}) collective-permute-start(f32[512,128]{1,0:T(8,128)S(1)} %get-tuple-element.12), channel_id=1, source_target_pairs={{0,16},{16,0},{1,17},{17,1},{2,18},{18,2},{3,19},{19,3},{4,20},{20... | collective-permute-start | bytes 786440 | tf_op jit(solution)/shard_map/ppermute | solution.py:448
  122.7 3.4 %collective-permute-start.1 = (f32[512,128]{1,0:T(8,128)S(1)}, f32[512,128]{1,0:T(8,128)S(1)}, u32[]{:S(2)}, u32[]{:S(2)}) collective-permute-start(f32[512,128]{1,0:T(8,128)S(1)} %bitcast.18), channel_id=1, source_target_pairs={{0,16},{16,0},{1,17},{17,1},{2,18},{18,2},{3,19},{19,3},{4,20},{20... | collective-permute-start | bytes 786440 | tf_op jit(solution)/shard_map/ppermute | solution.py:448
